TPU v7x, 32 devices: a whole 2x2x4 slice. The times are simulated.
32 devices in a mesh: grp: 2 (over x), chan: 16 (over z, y, core).
Axes of the slice: x: 2, y: 2, z: 4, core: 2. Of those that a mesh axis runs over, the one named last changes fastest.
Arguments:
- spectra: bfloat16 [2048, 2, 64, 512], P(('grp', 'chan')), parts along dimension 0, may hold values from -6 to 6
- valid: int32 [2048, 64], P(('grp', 'chan')), parts along dimension 0, may hold values 0 or 1
- sources: int32 [32], P('grp'), parts along dimension 0, may hold values from 0 to 1023
Outputs:
- smoothed: float32 [32, 1024, 1024], P('grp', 'chan'), parts along dimension 0
There are 2 independent parts, one for each index of `grp`. A program takes and returns all parts, laid end to end along the dimension named above; each array names one. Nothing has to cross between parts.
Inputs may be any that keep to these rules, and one draw needn't show every extreme that they name: `sources`: channel indices of the segment; repeats may occur.
All inputs are finite; a program needn't handle non-finite values. No bound on the sum of `valid` on one device may be relied on, other than what follows from the above.
Results may differ from a plain program's by a relative error of at most 0.0037.
Values may be sent and summed in bfloat16 or wider, within the bound.
A program may use at most 128 MiB of HBM per device.

v0:
```python
import functools

import jax
import jax.numpy as jnp
import numpy as np
from jax import lax
from jax.experimental import pallas as pl
from jax.experimental.pallas import tpu as pltpu
from jax.sharding import PartitionSpec as P

MESH = pl.DeviceIdType.MESH
HALO = 2
LAG = 4


def make_table(nbins, nlags):
    freq = np.arange(nbins, dtype=np.int64)
    phase = (freq[:, None] * np.arange(nlags, dtype=np.int64)[None, :]) % nlags
    angle = 2.0 * np.pi * phase / nlags
    weight = np.where(freq == 0, 1.0, 2.0) / nlags
    table = np.concatenate([weight[:, None] * np.cos(angle), -weight[:, None] * np.sin(angle)])
    return table.astype(np.float32).astype(jnp.bfloat16)


def pick_kernel(nsrc, src_ref, mask_ref, spec_ref, out_ref, edge_ref, buf, sems):
    nchan = spec_ref.shape[0]
    me = lax.axis_index("chan")
    spots, copies = [], []
    for row in range(nsrc + 2 * HALO):
        if row < nsrc:
            spot = src_ref[row] - me * nchan
        else:
            spot = row - nsrc if row < nsrc + HALO else nchan - 2 * HALO + row - nsrc
        held = jnp.clip(spot, 0, nchan - 1) if row < nsrc else spot
        copy = pltpu.make_async_copy(spec_ref.at[held], buf.at[row], sems.at[row])
        copy.start()
        spots.append(spot)
        copies.append(copy)
    mask = mask_ref[...]
    lane = lax.broadcasted_iota(jnp.int32, mask.shape, 1)
    for row, (spot, copy) in enumerate(zip(spots, copies)):
        column = jnp.sum(jnp.where(lane == spot, mask, 0.0), axis=1, keepdims=True)
        copy.wait()
        masked = (buf[row].astype(jnp.float32) * column).astype(out_ref.dtype)
        if row < nsrc:
            out_ref[row] = masked
        else:
            edge_ref[row - nsrc] = masked


def share_kernel(outer, inner, nchunk, pick_ref, edge_ref, out_ref, halo_ref, part, first, second,
                 ins, outs, send_sem, recv_sem, edge_send, edge_recv):
    half = nchunk // 2
    size = outer * inner * 2
    me = lax.axis_index("chan")
    core, chip = me % 2, me // 2
    j, i = chip % inner, chip // inner
    lines = ((j, inner, 2), (i, outer, 2 * inner))
    partner = me + 1 - 2 * core

    barrier = pltpu.get_barrier_semaphore()

    def greet(there):
        pl.semaphore_signal(barrier, inc=1, device_id={"chan": there}, device_id_type=MESH)

    greet(partner)
    count = jnp.int32(1)
    for pos, length, stride in lines + ((me, size, 1),):
        @pl.when(pos > 0)
        def _():
            greet(me - stride)

        @pl.when(pos < length - 1)
        def _():
            greet(me + stride)

        count = count + (pos > 0).astype(jnp.int32) + (pos < length - 1).astype(jnp.int32)
    pl.semaphore_wait(barrier, count)

    def remote(src, dst, kind, k, there):
        return pltpu.make_async_remote_copy(
            src_ref=src, dst_ref=dst, send_sem=send_sem.at[kind, k], recv_sem=recv_sem.at[kind, k],
            device_id={"chan": there}, device_id_type=MESH)

    def across(k):
        return remote(pick_ref.at[(1 - core) * half + k], part.at[k], 0, k, partner)

    def back(k):
        spot = core * half + k
        return remote(out_ref.at[spot], out_ref.at[spot], 1, k, partner)

    def hop(line, up, src, k):
        pos, length, stride = lines[line]
        kind = 2 + 2 * line + (0 if up else 1)
        there = me + stride if up else me - stride
        return remote(src, ins.at[kind - 2, k], kind, k, there)

    def to_after():
        return pltpu.make_async_remote_copy(
            src_ref=edge_ref.at[pl.ds(HALO, HALO)], dst_ref=halo_ref.at[pl.ds(0, HALO)],
            send_sem=edge_send.at[0], recv_sem=edge_recv.at[0],
            device_id={"chan": me + 1}, device_id_type=MESH)

    def to_before():
        return pltpu.make_async_remote_copy(
            src_ref=edge_ref.at[pl.ds(0, HALO)], dst_ref=halo_ref.at[pl.ds(HALO, HALO)],
            send_sem=edge_send.at[1], recv_sem=edge_recv.at[1],
            device_id={"chan": me - 1}, device_id_type=MESH)

    def begin(line, x, k):
        pos, length, _ = lines[line]
        if length == 1:
            return

        @pl.when(pos == 0)
        def _():
            hop(line, True, x.at[k], k).start()

        @pl.when(pos == length - 1)
        def _():
            hop(line, False, x.at[k], k).start()

    def guarded(k, also, run):
        @pl.when((k >= 0) & (k < half) & also)
        def _():
            run(k)

    def relay(line, x, t):
        pos, length, _ = lines[line]
        if length == 1:
            return

        def go(up):
            kind = 2 * line + (0 if up else 1)
            behind = pos - 1 if up else length - 2 - pos
            last = pos == (length - 1 if up else 0)
            first_one = pos == (0 if up else length - 1)

            def run(k):
                hop(line, up, x.at[k], k).wait_recv()
                if length > 2:
                    @pl.when(jnp.logical_not(last))
                    def _():
                        outs[kind, k] = x[k] + ins[kind, k]
                        hop(line, up, outs.at[kind, k], k).start()

            guarded(t - LAG * behind, jnp.logical_not(first_one), run)

        @pl.when(2 * pos < length)
        def _():
            go(True)
            go(False)

        @pl.when(2 * pos >= length)
        def _():
            go(False)
            go(True)

    def finish(line, x, k, total, at):
        pos, length, _ = lines[line]
        if length == 1:
            total[at] = x[k]
            return
        low, high = ins.at[2 * line], ins.at[2 * line + 1]

        @pl.when(pos == 0)
        def _():
            total[at] = x[k] + high[k]

        @pl.when(pos == length - 1)
        def _():
            total[at] = x[k] + low[k]

        if length > 2:
            @pl.when((pos > 0) & (pos < length - 1))
            def _():
                total[at] = x[k] + low[k] + high[k]

    def send_across(k, carry):
        across(k).start()
        return carry

    lax.fori_loop(0, half, send_across, 0)

    @pl.when(me == 0)
    def _():
        halo_ref[0:HALO] = jnp.zeros((HALO,) + halo_ref.shape[1:], halo_ref.dtype)

    @pl.when(me == size - 1)
    def _():
        halo_ref[HALO:] = jnp.zeros((HALO,) + halo_ref.shape[1:], halo_ref.dtype)

    ready = LAG
    passed = ready + LAG * max(inner - 2, 0)
    reached = passed + LAG
    done = reached + LAG * max(outer - 2, 0)

    def step(t, carry):
        def enter(k):
            across(k).wait_recv()
            first[k] = pick_ref[core * half + k] + part[k]
            begin(0, first, k)

        def turn(k):
            finish(0, first, k, second, k)
            begin(1, second, k)

        def leave(k):
            finish(1, second, k, out_ref, core * half + k)
            back(k).start()

        @pl.when(t == half)
        def _():
            @pl.when(me < size - 1)
            def _():
                to_after().start()

            @pl.when(me > 0)
            def _():
                to_before().start()

        guarded(t, True, enter)
        relay(0, first, t - ready)
        guarded(t - passed, True, turn)
        relay(1, second, t - reached)
        guarded(t - done, True, leave)
        return carry

    lax.fori_loop(0, half + done, step, 0)

    def close(k, carry):
        across(k).wait_send()
        other = (1 - core) * half + k
        remote(out_ref.at[other], out_ref.at[other], 1, k, partner).wait_recv()
        back(k).wait_send()
        for line, (pos, length, _) in enumerate(lines):
            if length == 1:
                continue

            @pl.when(pos < length - 1)
            def _():
                hop(line, True, first.at[k], k).wait_send()

            @pl.when(pos > 0)
            def _():
                hop(line, False, first.at[k], k).wait_send()

        return carry

    lax.fori_loop(0, half, close, 0)

    @pl.when(me < size - 1)
    def _():
        to_after().wait_send()
        to_before().wait_recv()

    @pl.when(me > 0)
    def _():
        to_before().wait_send()
        to_after().wait_recv()


def lag_kernel(nwin, nrow, sgroup, spec_ref, valid_ref, src_ref, halo_ref, table_ref, out_ref,
               chan_t, src_t, cross_t, lag):
    nchan, depth, fb = spec_ref.shape
    nsrc = src_ref.shape[0]
    nbins = table_ref.shape[0] // 2
    steps = nbins // fb
    at = pl.program_id(0)
    pitch, cpitch = fb + 1, 2 * nsrc + 1

    @pl.when(at < steps)
    def _():
        def turn(x):
            return jnp.transpose(x).astype(jnp.float32)

        for c in range(HALO):
            chan_t[c * pitch:c * pitch + fb] = turn(halo_ref[c])
            far = nchan + HALO + c
            chan_t[far * pitch:far * pitch + fb] = turn(halo_ref[HALO + c])

        def channel(c, carry):
            chan_t[pl.ds((c + HALO) * pitch, fb)] = (
                turn(spec_ref[c]) * valid_ref[pl.ds(c, 1)])
            return carry

        lax.fori_loop(0, nchan, channel, 0, unroll=4)
        sign = jnp.where(lax.broadcasted_iota(jnp.int32, (1, depth), 1) < nwin, -1.0, 1.0)

        def source(s, carry):
            x = turn(src_ref[s])
            src_t[pl.ds(s * pitch, fb)] = x
            src_t[pl.ds((s + nsrc) * pitch, fb)] = (
                pltpu.roll(x, nwin, axis=1) * sign)
            return carry

        lax.fori_loop(0, nsrc, source, 0, unroll=2)

        def one(f, carry):
            right = chan_t[pl.ds(f, nrow, stride=pitch)].astype(jnp.bfloat16)
            left = src_t[pl.ds(f, 2 * nsrc, stride=pitch)].astype(jnp.bfloat16)
            both = lax.dot_general(left, right, (((1,), (1,)), ((), ())),
                                   preferred_element_type=jnp.float32)
            row = (at * fb + f) * cpitch
            cross_t[pl.ds(row, 2 * nsrc), 0:nrow] = both * (1.0 / nwin)
            return carry

        lax.fori_loop(0, fb, one, 0, unroll=8)

    @pl.when(at >= steps)
    def _():
        group = at - steps
        rows = []
        for q in range(sgroup):
            s = group * sgroup + q
            re = cross_t[pl.ds(s, nbins, stride=cpitch)]
            im = cross_t[pl.ds(s + nsrc, nbins, stride=cpitch)]
            flat = jnp.concatenate([re, im], axis=0).astype(jnp.bfloat16)
            rows.append(jnp.transpose(flat)[0:nrow])
        lags = jnp.dot(jnp.concatenate(rows, axis=0), table_ref[...],
                       preferred_element_type=jnp.float32)
        for n in range(lag.shape[0]):
            lag[n] = lags[:, n * 128:(n + 1) * 128]
        for q in range(sgroup):
            base = q * nrow
            for n in range(lag.shape[0]):
                total = lag[n, base:base + nchan] + lag[n, base + 1:base + 1 + nchan]
                for k in range(2, 2 * HALO + 1):
                    total = total + lag[n, base + k:base + k + nchan]
                out_ref[q, :, n * 128:(n + 1) * 128] = total / (2 * HALO + 1.0)


def local(size, spectra, valid, sources):
    nchan, _, nwin, nbins = spectra.shape
    nsrc = sources.shape[0]
    depth, nlags = 2 * nwin, 2 * nbins
    spec = spectra.reshape(nchan, depth, nbins)
    flags = valid.astype(jnp.float32)
    flags2 = jnp.concatenate([flags, flags], axis=1)
    vmem = pl.BlockSpec(memory_space=pltpu.VMEM)

    picked, edges = pl.pallas_call(
        functools.partial(pick_kernel, nsrc),
        out_shape=[jax.ShapeDtypeStruct((nsrc, depth, nbins), jnp.bfloat16),
                   jax.ShapeDtypeStruct((2 * HALO, depth, nbins), jnp.bfloat16)],
        in_specs=[pl.BlockSpec(memory_space=pltpu.SMEM), vmem, pl.BlockSpec(memory_space=pltpu.MemorySpace.HBM)],
        out_specs=[vmem, vmem],
        scratch_shapes=[pltpu.VMEM((nsrc + 2 * HALO, depth, nbins), jnp.bfloat16),
                        pltpu.SemaphoreType.DMA((nsrc + 2 * HALO,))],
        compiler_params=pltpu.CompilerParams(vmem_limit_bytes=50 << 20),
        name="pick",
    )(sources, flags2.T, spec)

    chips = size // 2
    inner = 1
    while (2 * inner) ** 2 <= chips and chips % (2 * inner) == 0:
        inner *= 2
    outer = chips // inner
    cut = 4
    nchunk, crow = nsrc * cut, depth // cut
    half = nchunk // 2
    chunk = lambda *lead: pltpu.VMEM(lead + (crow, nbins), jnp.bfloat16)
    src, halo = pl.pallas_call(
        functools.partial(share_kernel, outer, inner, nchunk),
        out_shape=[jax.ShapeDtypeStruct((nchunk, crow, nbins), jnp.bfloat16),
                   jax.ShapeDtypeStruct((2 * HALO, depth, nbins), jnp.bfloat16)],
        in_specs=[vmem, vmem],
        out_specs=[vmem, vmem],
        scratch_shapes=[chunk(half), chunk(half), chunk(half), chunk(4, half), chunk(4, half),
                        pltpu.SemaphoreType.DMA((6, half)), pltpu.SemaphoreType.DMA((6, half)),
                        pltpu.SemaphoreType.DMA((2,)), pltpu.SemaphoreType.DMA((2,))],
        compiler_params=pltpu.CompilerParams(
            collective_id=0, has_side_effects=True, vmem_limit_bytes=24 << 20),
        name="share",
    )(picked.reshape(nchunk, crow, nbins), edges)
    src = src.reshape(nsrc, depth, nbins)

    fb = 128
    steps = nbins // fb
    sgroup = 4 if nsrc % 4 == 0 else 1
    nrow = -(-(nchan + 2 * HALO) // 16) * 16
    by_f = lambda at: (0, 0, jnp.minimum(at, steps - 1))
    return pl.pallas_call(
        functools.partial(lag_kernel, nwin, nrow, sgroup),
        grid=(steps + nsrc // sgroup,),
        out_shape=jax.ShapeDtypeStruct((nsrc, nchan, nlags), jnp.float32),
        in_specs=[pl.BlockSpec((nchan, depth, fb), by_f),
                  pl.BlockSpec((nchan, depth), lambda at: (0, 0)),
                  pl.BlockSpec((nsrc, depth, fb), by_f),
                  pl.BlockSpec((2 * HALO, depth, fb), by_f),
                  pl.BlockSpec((nlags, nlags), lambda at: (0, 0))],
        out_specs=pl.BlockSpec((sgroup, nchan, nlags), lambda at: (jnp.maximum(at - steps, 0), 0, 0)),
        scratch_shapes=[pltpu.VMEM((nrow * (fb + 1), depth), jnp.float32),
                        pltpu.VMEM((2 * nsrc * (fb + 1), depth), jnp.float32),
                        pltpu.VMEM((nbins * (2 * nsrc + 1), 128), jnp.float32),
                        pltpu.VMEM((nlags // 128, sgroup * nrow, 128), jnp.float32)],
        compiler_params=pltpu.CompilerParams(vmem_limit_bytes=50 << 20),
        name="lags",
    )(spec, flags2, src, halo, jnp.asarray(make_table(nbins, nlags)))


def solution(mesh):
    in_specs = (P(("grp", "chan"), None, None, None), P(("grp", "chan"), None), P("grp"))
    out_specs = P("grp", "chan", None)
    return jax.shard_map(functools.partial(local, mesh.shape["chan"]), mesh=mesh,
                         in_specs=in_specs, out_specs=out_specs, check_vma=False)
```

profile of v0, /device:TPU:0, one launch (start us, length us, event | category | flops | bytes accessed | tf_op | source)
XLA Modules:
  0.0 83.8 jit_solution(10606673527916478182)
XLA Ops:
  0.0 0.8 convert_element_type.3
  0.8 0.1 fusion
  0.8 0.1 copy.5.mask_ref
  0.9 0.0 copy-start
  1.0 0.7 copy-done
  1.6 3.4 %pick.1 = (bf16[16,128,512]{2,1,0:T(8,128)(2,1)S(1)}, bf16[4,128,512]{2,1,0:T(8,128)(2,1)S(1)}) custom-call(s32[16]{0:T(128)S(1)} %copy-done, f32[128,64]{1,0:T(8,128)S(1)} %copy.5.mask_ref, bf16[64,128,512]{2,1,0:T(8,128)(2,1)} %bitcast.7), custom_call_target="tpu_custom_call" | custom-call | tf_op jit(solution)/shard_map/pick/pallas_call | solution.py:342
  5.0 46.7 %share.1 = (bf16[64,32,512]{2,1,0:T(8,128)(2,1)S(1)}, bf16[4,128,512]{2,1,0:T(8,128)(2,1)S(1)}) custom-call(bf16[64,32,512]{2,1,0:T(8,128)(2,1)S(1)} %bitcast.6, bf16[4,128,512]{2,1,0:T(8,128)(2,1)S(1)} %get-tuple-element.10.edge_ref), custom_call_target="tpu_custom_call" | custom-call | tf_op jit(solution)/shard_map/share/pallas_call | solution.py:363
  51.8 32.1 %lags.1 = f32[16,64,1024]{2,1,0:T(8,128)} custom-call(bf16[64,128,512]{2,1,0:T(8,128)(2,1)} %bitcast.8, f32[64,128]{1,0:T(8,128)S(1)} %get-tuple-element.14.valid_ref, bf16[16,128,512]{2,1,0:T(8,128)(2,1)S(1)} %bitcast.5, bf16[4,128,512]{2,1,0:T(8,128)(2,1)S(1)} %get-tuple-element.12.halo_ref, bf16[1024,1024]{1,0:T(8,128)(2,1)} %constant.2.clone.table_ref), custom_call_target="tpu_custom_call" | custom-call | tf_op jit(solution)/shard_map/lags/pallas_call | solution.py:383
Async XLA Ops:
  0.9 0.7 copy-start
where the time goes:
time: 84 us; the launch traced here: 83.8 us
  Pallas kernels  82.2 us (98%)
  other arithmetic  0.84 us (1%)
    pallas_call x1, Pallas kernels, local(): pl.pallas_call(functools.partial(share_kernel, outer, inner, nchunk), out...  46.7 us
    pallas_call x1, Pallas kernels, local(): pl.pallas_call(functools.partial(lag_kernel, nwin, nrow, sgroup), grid=(s...  32.1 us
    pallas_call x1, Pallas kernels, local(): pl.pallas_call(functools.partial(pick_kernel, nsrc), out_shape=[jax.Shape...  3.43 us

commit v1 on v0

v1 whole, which is shorter than its diff:
```python
import functools

import jax
import jax.numpy as jnp
import numpy as np
from jax import lax
from jax.experimental import pallas as pl
from jax.experimental.pallas import tpu as pltpu
from jax.sharding import PartitionSpec as P

MESH = pl.DeviceIdType.MESH
HALO = 2
LAG = 4
ENTER = 2
SETTLE = 2
LOADED = 4
FB = 128
ACROSS, BACK, IN_UP, IN_DOWN, ON_UP, ON_DOWN, OUT_UP, OUT_DOWN = range(8)
KINDS = 8


def make_table(nbins, nlags):
    freq = np.arange(nbins, dtype=np.int64)
    phase = (freq[:, None] * np.arange(nlags, dtype=np.int64)[None, :]) % nlags
    angle = 2.0 * np.pi * phase / nlags
    weight = np.where(freq == 0, 1.0, 2.0) / nlags
    table = np.concatenate([weight[:, None] * np.cos(angle), -weight[:, None] * np.sin(angle)])
    return table.astype(np.float32).astype(jnp.bfloat16)


def cross_kernel(outer, inner, nrow, src_ref, valid_ref, spec_ref, flat_ref,
                 first, spec, halo, halo_valid, flags, plane, give, own, part, inward, along, passed, gathered,
                 chan_t, src_t, cross_t, load_sem, send_sem, recv_sem, edge_send, edge_recv):
    nblk, nchan, depth, _ = spec.shape
    nsrc, nwin, _ = plane.shape
    per = nsrc // 2
    n = nblk * per
    size = outer * inner * 2
    me = lax.axis_index("chan")
    core, chip = me % 2, me // 2
    j, i = chip % inner, chip // inner
    line_j, line_i = (j, inner, 2), (i, outer, 2 * inner)
    teeth, spine = (line_j, line_i), (line_i, line_j)
    partner = me + 1 - 2 * core
    pitch, cpitch = FB + 1, 2 * nsrc + 1

    def reach(q):
        length = teeth[q][1]
        return length - 1 if q == 0 else length - 1 - (length - 1) // 2

    def root(q, k):
        length = teeth[q][1]
        if length == 1:
            return 0
        return k % length if q == 0 else (length - 1) // 2 + k % 2

    rooted = [ENTER + LAG * reach(q) for q in range(2)]
    summed = [rooted[q] + LAG * (spine[q][1] - 1) for q in range(2)]
    settled = max(summed[q] + LAG * reach(q) for q in range(2)) + SETTLE
    turn_at = settled - per

    def load(b):
        return pltpu.make_async_copy(spec_ref.at[:, :, pl.ds(b * FB, FB)], spec.at[b], load_sem.at[1 + b])

    load_first = pltpu.make_async_copy(spec_ref.at[:, :, pl.ds(0, FB)], first, load_sem.at[0])
    load_first.start()
    for b in range(nblk):
        load(b).start()

    barrier = pltpu.get_barrier_semaphore()

    def greet(there):
        pl.semaphore_signal(barrier, inc=1, device_id={"chan": there}, device_id_type=MESH)

    greet(partner)
    count = jnp.int32(1)
    for pos, length, stride in (line_j, line_i, (me, size, 1)):
        @pl.when(pos > 0)
        def _():
            greet(me - stride)

        @pl.when(pos < length - 1)
        def _():
            greet(me + stride)

        count = count + (pos > 0).astype(jnp.int32) + (pos < length - 1).astype(jnp.int32)

    raw = valid_ref[...].astype(jnp.float32)
    flags[...] = jnp.concatenate([raw, raw], axis=1)
    by_window = jnp.transpose(flags[...])[0:nwin].astype(jnp.bfloat16)
    place = lax.broadcasted_iota(jnp.int32, (nchan, FB), 0)
    for s in range(nsrc):
        hot = (place == src_ref[s] - me * nchan).astype(jnp.bfloat16)
        plane[s] = jnp.dot(by_window, hot, preferred_element_type=jnp.float32).astype(jnp.bfloat16)

    pl.semaphore_wait(barrier, count)

    def edges(up):
        there = me + 1 if up else me - 1
        side, rows = (0, nchan - HALO) if up else (1, 0)
        eight = nchan - 8 if up else 0
        return [pltpu.make_async_remote_copy(
                    src_ref=spec_ref.at[pl.ds(rows, HALO)], dst_ref=halo.at[pl.ds(side * HALO, HALO)],
                    send_sem=edge_send.at[side, 0], recv_sem=edge_recv.at[side, 0],
                    device_id={"chan": there}, device_id_type=MESH),
                pltpu.make_async_remote_copy(
                    src_ref=valid_ref.at[pl.ds(eight, 8)], dst_ref=halo_valid.at[side],
                    send_sem=edge_send.at[side, 1], recv_sem=edge_recv.at[side, 1],
                    device_id={"chan": there}, device_id_type=MESH)]

    @pl.when(me < size - 1)
    def _():
        for copy in edges(True):
            copy.start()

    @pl.when(me > 0)
    def _():
        for copy in edges(False):
            copy.start()

    def remote(src, dst, kind, q, k, there):
        return pltpu.make_async_remote_copy(
            src_ref=src, dst_ref=dst, send_sem=send_sem.at[kind, q, k], recv_sem=recv_sem.at[kind, q, k],
            device_id={"chan": there}, device_id_type=MESH)

    def spot(q, k, half):
        return (2 * k + q) * 2 + half

    def across(q, k):
        return remote(give.at[q, k], part.at[q, k], ACROSS, q, k, partner)

    def back(q, k, half):
        at = spot(q, k, half)
        return remote(gathered.at[at], gathered.at[at], BACK, q, k, partner)

    def toward(q, up, k):
        there = me + teeth[q][2] if up else me - teeth[q][2]
        return remote(own.at[q, k], inward.at[0 if up else 1, q, k], IN_UP if up else IN_DOWN, q, k, there)

    def onward(q, up, k, src):
        there = me + spine[q][2] if up else me - spine[q][2]
        return remote(src, along.at[0 if up else 1, q, k], ON_UP if up else ON_DOWN, q, k, there)

    def outward(q, up, k):
        there = me + teeth[q][2] if up else me - teeth[q][2]
        at = spot(q, k, core)
        return remote(gathered.at[at], gathered.at[at], OUT_UP if up else OUT_DOWN, q, k, there)

    def prepare(block, s, q, k):
        held = jnp.clip(src_ref[s] - me * nchan, 0, nchan - 1)
        mask = plane[s]
        give[q, k] = block[held, pl.ds((1 - core) * nwin, nwin)] * mask
        own[q, k] = block[held, pl.ds(core * nwin, nwin)] * mask
        across(q, k).start()

    def guarded(k, also, run):
        @pl.when((k >= 0) & (k < n) & also)
        def _():
            run(k)

    def enter(q, k):
        pos, length, _ = teeth[q]
        across(q, k).wait_recv()
        own[q, k] = own[q, k] + part[q, k]
        if length > 1:
            @pl.when((pos == 0) & (root(q, k) > 0))
            def _():
                toward(q, True, k).start()

            @pl.when((pos == length - 1) & (root(q, k) < length - 1))
            def _():
                toward(q, False, k).start()

    def relay_in(q, t):
        pos, length, _ = teeth[q]
        if length <= 2:
            return

        def run(up):
            def go(k):
                @pl.when(pos < root(q, k) if up else pos > root(q, k))
                def _():
                    toward(q, up, k).wait_recv()
                    own[q, k] = own[q, k] + inward[0 if up else 1, q, k]
                    toward(q, up, k).start()

            steps = pos if up else length - 1 - pos
            guarded(t - LAG * steps, steps > 0, go)

        run(True)
        run(False)

    def reach_root(q, k):
        pos, length, _ = teeth[q]
        at, span, _ = spine[q]

        @pl.when(pos == root(q, k))
        def _():
            if length > 1:
                @pl.when(pos > 0)
                def _():
                    toward(q, True, k).wait_recv()
                    own[q, k] = own[q, k] + inward[0, q, k]

                @pl.when(pos < length - 1)
                def _():
                    toward(q, False, k).wait_recv()
                    own[q, k] = own[q, k] + inward[1, q, k]
            if span > 1:
                @pl.when(at == 0)
                def _():
                    onward(q, True, k, own.at[q, k]).start()

                @pl.when(at == span - 1)
                def _():
                    onward(q, False, k, own.at[q, k]).start()

    def relay_on(q, t):
        pos, length, _ = teeth[q]
        at, span, _ = spine[q]
        if span == 1:
            return

        def run(up):
            def go(k):
                @pl.when(pos == root(q, k))
                def _():
                    onward(q, up, k, own.at[q, k]).wait_recv()
                    if span > 2:
                        @pl.when(at < span - 1 if up else at > 0)
                        def _():
                            passed[0 if up else 1, q, k] = own[q, k] + along[0 if up else 1, q, k]
                            onward(q, up, k, passed.at[0 if up else 1, q, k]).start()

            steps = at if up else span - 1 - at
            guarded(t - LAG * steps, steps > 0, go)

        run(True)
        run(False)

    def finish(q, k):
        pos, length, _ = teeth[q]
        at, span, _ = spine[q]

        @pl.when(pos == root(q, k))
        def _():
            to = spot(q, k, core)
            if span == 1:
                gathered[to] = own[q, k]
            else:
                @pl.when(at == 0)
                def _():
                    gathered[to] = own[q, k] + along[1, q, k]

                @pl.when(at == span - 1)
                def _():
                    gathered[to] = own[q, k] + along[0, q, k]

                if span > 2:
                    @pl.when((at > 0) & (at < span - 1))
                    def _():
                        gathered[to] = own[q, k] + along[0, q, k] + along[1, q, k]
            if length > 1:
                @pl.when(pos < length - 1)
                def _():
                    outward(q, True, k).start()

                @pl.when(pos > 0)
                def _():
                    outward(q, False, k).start()
            back(q, k, core).start()

    def spread(q, t):
        pos, length, _ = teeth[q]
        if length == 1:
            return

        def run(far, up):
            def go(k):
                @pl.when(pos - root(q, k) == (far if up else -far))
                def _():
                    outward(q, up, k).wait_recv()
                    if far < reach(q):
                        @pl.when(pos < length - 1 if up else pos > 0)
                        def _():
                            outward(q, up, k).start()
                    back(q, k, core).start()

            guarded(t - LAG * far, True, go)

        for far in range(reach(q), 0, -1):
            run(far, True)
            run(far, False)

    def sent(q, k):
        pos, length, _ = teeth[q]
        at, span, _ = spine[q]
        across(q, k).wait_send()
        back(q, k, core).wait_send()
        if length > 1:
            @pl.when(pos < root(q, k))
            def _():
                toward(q, True, k).wait_send()

            @pl.when(pos > root(q, k))
            def _():
                toward(q, False, k).wait_send()

            @pl.when((pos >= root(q, k)) & (pos < length - 1))
            def _():
                outward(q, True, k).wait_send()

            @pl.when((pos <= root(q, k)) & (pos > 0))
            def _():
                outward(q, False, k).wait_send()
        if span > 1:
            @pl.when((pos == root(q, k)) & (at < span - 1))
            def _():
                onward(q, True, k, own.at[q, k]).wait_send()

            @pl.when((pos == root(q, k)) & (at > 0))
            def _():
                onward(q, False, k, own.at[q, k]).wait_send()

    sign = jnp.where(lax.broadcasted_iota(jnp.int32, (1, depth), 1) < nwin, -1.0, 1.0)

    def settle(k):
        b, pair = k // per, k % per
        base = (b % 2) * (2 * nsrc * pitch)
        for q in range(2):
            back(q, k, 1 - core).wait_recv()
        for q in range(2):
            at = spot(q, k, 0)
            x = jnp.transpose(jnp.concatenate([gathered[at], gathered[at + 1]], axis=0)).astype(jnp.float32)
            s = 2 * pair + q
            src_t[pl.ds(base + s * pitch, FB)] = x
            src_t[pl.ds(base + (s + nsrc) * pitch, FB)] = pltpu.roll(x, nwin, axis=1) * sign
        for q in range(2):
            sent(q, k)

    def turn(k):
        b, lot = k // per, k % per
        base = (b % 3) * (nrow * pitch)
        count = nchan // per
        for u in range(count):
            c = lot * count + u
            x = jnp.transpose(spec[b, c]).astype(jnp.float32) * flags[pl.ds(c, 1)]
            chan_t[pl.ds(base + (c + HALO) * pitch, FB)] = x

        @pl.when(lot == 0)
        def _():
            column = pl.multiple_of(b * FB, FB)
            for h in range(2 * HALO):
                row = halo_valid[h // HALO][(8 - HALO + h) if h < HALO else (h - HALO)][None].astype(jnp.float32)
                row = jnp.concatenate([row, row], axis=1)
                x = jnp.transpose(halo[h, :, pl.ds(column, FB)]).astype(jnp.float32) * row
                c = h if h < HALO else nchan + h
                chan_t[pl.ds(base + c * pitch, FB)] = x

    def correlate(b, f):
        right = chan_t[pl.ds((b % 3) * (nrow * pitch) + f, nrow, stride=pitch)].astype(jnp.bfloat16)
        left = src_t[pl.ds((b % 2) * (2 * nsrc * pitch) + f, 2 * nsrc, stride=pitch)].astype(jnp.bfloat16)
        both = lax.dot_general(left, right, (((1,), (1,)), ((), ())), preferred_element_type=jnp.float32)
        cross_t[pl.ds((b % 2) * (FB * cpitch) + f * cpitch, 2 * nsrc), 0:nrow] = both

    ahead = (lax.broadcasted_iota(jnp.int32, (nchan, FB), 1)
             - lax.broadcasted_iota(jnp.int32, (nchan, FB), 0))
    band = ((ahead >= 0) & (ahead <= 2 * HALO)).astype(jnp.bfloat16)

    def smooth(b, s):
        base = (b % 2) * (FB * cpitch)
        re = cross_t[pl.ds(base + s, FB, stride=cpitch)]
        im = cross_t[pl.ds(base + s + nsrc, FB, stride=cpitch)]
        flat = jnp.concatenate([re, im], axis=0).astype(jnp.bfloat16)
        total = lax.dot_general(band, flat, (((1,), (1,)), ((), ())),
                                preferred_element_type=jnp.float32).astype(jnp.bfloat16)
        rows = pl.ds(pl.multiple_of(s * nchan, nchan), nchan)
        flat_ref[rows, pl.ds(pl.multiple_of(b * FB, FB), FB)] = total[:, 0:FB]
        flat_ref[rows, pl.ds(pl.multiple_of((nblk + b) * FB, FB), FB)] = total[:, FB:]

    load_first.wait()

    def prepare_first(k, carry):
        for q in range(2):
            prepare(first, 2 * k + q, q, k)
        return carry

    lax.fori_loop(0, per, prepare_first, 0, unroll=True)

    @pl.when(me == 0)
    def _():
        halo[0:HALO] = jnp.zeros((HALO,) + halo.shape[1:], halo.dtype)
        halo_valid[0] = jnp.zeros(halo_valid.shape[1:], halo_valid.dtype)

    @pl.when(me == size - 1)
    def _():
        halo[HALO:] = jnp.zeros((HALO,) + halo.shape[1:], halo.dtype)
        halo_valid[1] = jnp.zeros(halo_valid.shape[1:], halo_valid.dtype)

    def step(t, carry):
        @pl.when(t == LOADED)
        def _():
            for b in range(nblk):
                load(b).wait()

        @pl.when(t == LOADED + 1)
        def _():
            cross_t[...] = jnp.zeros(cross_t.shape, cross_t.dtype)
            pads = (nrow - nchan - 2 * HALO) * pitch
            for slot in range(3):
                chan_t[slot * nrow * pitch + (nrow * pitch - pads):(slot + 1) * nrow * pitch] = (
                    jnp.zeros((pads, depth), jnp.float32))

        @pl.when(t == turn_at)
        def _():
            @pl.when(me > 0)
            def _():
                for copy in edges(True):
                    copy.wait_recv()

            @pl.when(me < size - 1)
            def _():
                for copy in edges(False):
                    copy.wait_recv()

        for q in range(2):
            spread(q, t - summed[q])
            relay_on(q, t - rooted[q])
            guarded(t - summed[q], True, functools.partial(finish, q))
            guarded(t - rooted[q], True, functools.partial(reach_root, q))
            relay_in(q, t - ENTER)
            guarded(t - ENTER, True, functools.partial(enter, q))

        def prepare_later(k):
            for q in range(2):
                s = 2 * (k % per) + q
                prepare(spec.at[k // per], s, q, k)

        guarded(t, t >= per, prepare_later)
        guarded(t - turn_at, True, turn)
        guarded(t - settled, True, settle)

        at = t - settled - per

        @pl.when((at >= 0) & (at < n - per))
        def _():
            b, lot = at // per, at % per
            for u in range(FB // per):
                correlate(b, lot * (FB // per) + u)

        also = at - per

        @pl.when((also >= 0) & (also < n - 2 * per))
        def _():
            b, lot = also // per, also % per
            for u in range(2):
                smooth(b, lot * 2 + u)

        return carry

    lax.fori_loop(0, n + settled, step, 0)

    def rest(u, carry):
        for v in range(32):
            correlate(nblk - 1, u * 32 + v)
        return carry

    lax.fori_loop(0, FB // 32, rest, 0)
    for b in range(max(nblk - 2, 0), nblk):
        def last(s, carry):
            smooth(b, s)
            return carry

        lax.fori_loop(0, nsrc, last, 0, unroll=4)

    @pl.when(me < size - 1)
    def _():
        for copy in edges(True):
            copy.wait_send()

    @pl.when(me > 0)
    def _():
        for copy in edges(False):
            copy.wait_send()


def lag_kernel(scale, flat_ref, table_ref, out_ref):
    lags = jnp.dot(flat_ref[...], table_ref[...], preferred_element_type=jnp.float32)
    out_ref[...] = lags * scale


def local(size, spectra, valid, sources):
    nchan, _, nwin, nbins = spectra.shape
    nsrc = sources.shape[0]
    depth, nlags = 2 * nwin, 2 * nbins
    spec = spectra.reshape(nchan, depth, nbins)
    vmem = pl.BlockSpec(memory_space=pltpu.VMEM)

    chips = size // 2
    inner = 1
    while (2 * inner) ** 2 <= chips and chips % (2 * inner) == 0:
        inner *= 2
    outer = chips // inner
    nblk = nbins // FB
    n = nblk * nsrc // 2
    nrow = -(-(nchan + 2 * HALO) // 16) * 16
    pitch, cpitch = FB + 1, 2 * nsrc + 1
    chunks = lambda *lead: pltpu.VMEM(lead + (2, n, nwin, FB), jnp.bfloat16)
    flat = pl.pallas_call(
        functools.partial(cross_kernel, outer, inner, nrow),
        out_shape=jax.ShapeDtypeStruct((nsrc * nchan, nlags), jnp.bfloat16),
        in_specs=[pl.BlockSpec(memory_space=pltpu.SMEM), vmem, pl.BlockSpec(memory_space=pltpu.MemorySpace.HBM)],
        out_specs=vmem,
        scratch_shapes=[pltpu.VMEM((nchan, depth, FB), jnp.bfloat16),
                        pltpu.VMEM((nblk, nchan, depth, FB), jnp.bfloat16),
                        pltpu.VMEM((2 * HALO, depth, nbins), jnp.bfloat16),
                        pltpu.VMEM((2, 8, nwin), jnp.int32),
                        pltpu.VMEM((nchan, depth), jnp.float32),
                        pltpu.VMEM((nsrc, nwin, FB), jnp.bfloat16),
                        chunks(), chunks(), chunks(), chunks(2), chunks(2), chunks(2),
                        pltpu.VMEM((nblk * nsrc * 2, nwin, FB), jnp.bfloat16),
                        pltpu.VMEM((3 * nrow * pitch, depth), jnp.float32),
                        pltpu.VMEM((2 * 2 * nsrc * pitch, depth), jnp.float32),
                        pltpu.VMEM((2 * FB * cpitch, FB), jnp.float32),
                        pltpu.SemaphoreType.DMA((1 + nblk,)),
                        pltpu.SemaphoreType.DMA((KINDS, 2, n)), pltpu.SemaphoreType.DMA((KINDS, 2, n)),
                        pltpu.SemaphoreType.DMA((2, 2)), pltpu.SemaphoreType.DMA((2, 2))],
        compiler_params=pltpu.CompilerParams(
            collective_id=0, has_side_effects=True, vmem_limit_bytes=54 << 20),
        name="cross",
    )(sources, valid, spec)

    rows = nsrc * nchan // 4
    lags = pl.pallas_call(
        functools.partial(lag_kernel, 1.0 / (nwin * (2 * HALO + 1.0))),
        grid=(4,),
        out_shape=jax.ShapeDtypeStruct((nsrc * nchan, nlags), jnp.float32),
        in_specs=[pl.BlockSpec((rows, nlags), lambda at: (at, 0)),
                  pl.BlockSpec((nlags, nlags), lambda at: (0, 0))],
        out_specs=pl.BlockSpec((rows, nlags), lambda at: (at, 0)),
        compiler_params=pltpu.CompilerParams(vmem_limit_bytes=24 << 20),
        name="lags",
    )(flat, jnp.asarray(make_table(nbins, nlags)))
    return lags.reshape(nsrc, nchan, nlags)


def solution(mesh):
    in_specs = (P(("grp", "chan"), None, None, None), P(("grp", "chan"), None), P("grp"))
    out_specs = P("grp", "chan", None)
    return jax.shard_map(functools.partial(local, mesh.shape["chan"]), mesh=mesh,
                         in_specs=in_specs, out_specs=out_specs, check_vma=False)
```

time: 84 us -> 75.5 us (0.90)
  Pallas kernels: 82.2 us -> 73.8 us
  local copies, waits for them, and re-layouts: 0.75 us -> 1.59 us
  other arithmetic: 0.84 us -> 0 us
    pallas_call x3 -> x2, Pallas kernels: 82.2 us -> 73.8 us  [the longest x1 69.7 us: local(): pl.pallas_call(functools.partial(cross_kernel, outer, inner, nrow), out_s...]
    unnamed x2 -> x4, local copies, waits for them, and re-layouts: 0.65 us -> 1.59 us
where the time goes in v1:
time: 75.5 us; the launch traced here: 75.4 us
  Pallas kernels  73.8 us (98%)
  local copies, waits for them, and re-layouts  1.59 us (2%)
    pallas_call x1, Pallas kernels, local(): pl.pallas_call(functools.partial(cross_kernel, outer, inner, nrow), out_s...  69.7 us
    pallas_call x1, Pallas kernels, local(): pl.pallas_call(functools.partial(lag_kernel, 1.0 / (nwin * (2 * HALO + 1....  4.1 us
    unnamed x4, local copies, waits for them, and re-layouts  1.59 us

profile of v1, /device:TPU:0, one launch (start us, length us, event | category | flops | bytes accessed | tf_op | source)
XLA Modules:
  0.0 75.4 jit_solution(3686807215986642168)
XLA Ops:
  0.0 0.0 copy-start.1
  0.0 69.7 %cross.1.flat_ref = bf16[1024,1024]{1,0:T(8,128)(2,1)} custom-call(s32[16]{0:T(128)} %src_ref.1, s32[64,64]{1,0:T(8,128)} %valid_ref.1, bf16[64,128,512]{2,1,0:T(8,128)(2,1)} %bitcast.2), custom_call_target="tpu_custom_call" | custom-call | tf_op jit(solution)/shard_map/cross/pallas_call | solution.py:509
  69.7 0.0 copy-done.1
  69.7 0.0 copy-start
  69.7 1.6 %copy-done = bf16[1024,1024]{1,0:T(8,128)(2,1)S(1)} copy-done((bf16[1024,1024]{1,0:T(8,128)(2,1)S(1)}, bf16[1024,1024]{1,0:T(8,128)(2,1)}, u32[]{:S(2)}) %copy-start) | copy-done | bytes 2097176
  71.3 4.1 %lags.1 = f32[1024,1024]{1,0:T(8,128)} custom-call(bf16[1024,1024]{1,0:T(8,128)(2,1)S(1)} %copy-done, bf16[1024,1024]{1,0:T(8,128)(2,1)S(1)} %copy-done.1), custom_call_target="tpu_custom_call" | custom-call | tf_op jit(solution)/shard_map/lags/pallas_call | solution.py:534
Async XLA Ops:
  0.0 69.7 %copy-start.1 = (bf16[1024,1024]{1,0:T(8,128)(2,1)S(1)}, bf16[1024,1024]{1,0:T(8,128)(2,1)}, u32[]{:S(2)}) copy-start(bf16[1024,1024]{1,0:T(8,128)(2,1)} %constant.2.clone.table_ref) | copy-start | bytes 6291460
  69.7 1.6 %copy-start = (bf16[1024,1024]{1,0:T(8,128)(2,1)S(1)}, bf16[1024,1024]{1,0:T(8,128)(2,1)}, u32[]{:S(2)}) copy-start(bf16[1024,1024]{1,0:T(8,128)(2,1)} %cross.1.flat_ref) | copy-start | bytes 6291460

commit v2 on v1

v2 whole, which is shorter than its diff:
```python
import functools

import jax
import jax.numpy as jnp
import numpy as np
from jax import lax
from jax.experimental import pallas as pl
from jax.experimental.pallas import tpu as pltpu
from jax.sharding import PartitionSpec as P

MESH = pl.DeviceIdType.MESH
HALO = 2
LAG = 3
ENTER = 2
SETTLE = 2
LOADED = 4
EARLY = 5
FB = 128
MANY = 2
IN_UP, IN_DOWN, ON_UP, ON_DOWN, OUT_UP, OUT_DOWN = range(6)


def make_table(nbins, nlags):
    freq = np.arange(nbins, dtype=np.int64)
    phase = (freq[:, None] * np.arange(nlags, dtype=np.int64)[None, :]) % nlags
    angle = 2.0 * np.pi * phase / nlags
    weight = np.where(freq == 0, 1.0, 2.0) / nlags
    table = np.concatenate([weight[:, None] * np.cos(angle), -weight[:, None] * np.sin(angle)])
    return table.astype(np.float32).astype(jnp.bfloat16)


def cross_kernel(outer, inner, nrow, src_ref, valid_ref, spec_ref, flat_ref,
                 first, spec, halo, halo_valid, flags, plane, give, own, part, inward, along, passed, gathered,
                 chan_t, src_t, cross_t, load_sem, pair_send, pair_recv, send_sem, recv_sem, edge_send, edge_recv):
    nblk, nchan, _, nwin, _ = spec.shape
    nsrc, depth = plane.shape[0], 2 * nwin
    n, _, many, _, _ = give.shape
    per = n // nblk
    size = outer * inner * 2
    me = lax.axis_index("chan")
    core, chip = me % 2, me // 2
    j, i = chip % inner, chip // inner
    line_j, line_i = (j, inner, 2), (i, outer, 2 * inner)
    teeth, spine = (line_j, line_i), (line_i, line_j)
    partner = me + 1 - 2 * core
    pitch, cpitch = FB + 1, 2 * nsrc + 1

    def root(q, odd):
        length = teeth[q][1]
        return 0 if length == 1 else (length - 1) // 2 + odd

    reach = [max(root(q, 1), teeth[q][1] - 1 - root(q, 0)) for q in range(2)]
    rooted = [ENTER + LAG * reach[q] for q in range(2)]
    summed = [rooted[q] + LAG * (spine[q][1] - 1) for q in range(2)]
    spread_at = max(summed[q] + LAG * reach[q] for q in range(2))
    settled = spread_at + SETTLE
    turn_at = settled - per
    at_root = [[teeth[q][0] == root(q, odd) for odd in range(2)] for q in range(2)]

    def load(b):
        return pltpu.make_async_copy(spec_ref.at[:, :, :, pl.ds(b * FB, FB)], spec.at[b], load_sem.at[1 + b])

    load_first = pltpu.make_async_copy(spec_ref.at[:, :, :, pl.ds(0, FB)], first, load_sem.at[0])
    load_first.start()
    for b in range(nblk):
        load(b).start()

    barrier = pltpu.get_barrier_semaphore()

    def greet(there):
        pl.semaphore_signal(barrier, inc=1, device_id={"chan": there}, device_id_type=MESH)

    greet(partner)
    count = jnp.int32(1)
    for pos, length, stride in (line_j, line_i, (me, size, 1)):
        @pl.when(pos > 0)
        def _():
            greet(me - stride)

        @pl.when(pos < length - 1)
        def _():
            greet(me + stride)

        count = count + (pos > 0).astype(jnp.int32) + (pos < length - 1).astype(jnp.int32)

    raw = valid_ref[...].astype(jnp.float32)
    flags[...] = jnp.concatenate([raw, raw], axis=1)
    by_window = jnp.transpose(flags[...])[0:nwin].astype(jnp.bfloat16)
    place = lax.broadcasted_iota(jnp.int32, (nchan, FB), 0)
    for s in range(nsrc):
        hot = (place == src_ref[s] - me * nchan).astype(jnp.bfloat16)
        plane[s] = jnp.dot(by_window, hot, preferred_element_type=jnp.float32).astype(jnp.bfloat16)

    pl.semaphore_wait(barrier, count)

    def edge_flags(up):
        side, eight = (0, nchan - 8) if up else (1, 0)
        return pltpu.make_async_remote_copy(
            src_ref=valid_ref.at[pl.ds(eight, 8)], dst_ref=halo_valid.at[side],
            send_sem=edge_send.at[side, nblk], recv_sem=edge_recv.at[side, nblk],
            device_id={"chan": me + 1 if up else me - 1}, device_id_type=MESH)

    def edge(up, b):
        side, rows = (0, nchan - HALO) if up else (1, 0)
        return pltpu.make_async_remote_copy(
            src_ref=spec_ref.at[pl.ds(rows, HALO), :, :, pl.ds(b * FB, FB)], dst_ref=halo.at[side, b],
            send_sem=edge_send.at[side, b], recv_sem=edge_recv.at[side, b],
            device_id={"chan": me + 1 if up else me - 1}, device_id_type=MESH)

    def to_neighbours(act, blocks=()):
        @pl.when(me < size - 1)
        def _():
            for copy in [edge(True, b) for b in blocks] or [edge_flags(True)]:
                act(copy)

        @pl.when(me > 0)
        def _():
            for copy in [edge(False, b) for b in blocks] or [edge_flags(False)]:
                act(copy)

    def from_neighbours(blocks=()):
        @pl.when(me > 0)
        def _():
            for copy in [edge(True, b) for b in blocks] or [edge_flags(True)]:
                copy.wait_recv()

        @pl.when(me < size - 1)
        def _():
            for copy in [edge(False, b) for b in blocks] or [edge_flags(False)]:
                copy.wait_recv()

    to_neighbours(lambda copy: copy.start())

    def across(k):
        return pltpu.make_async_remote_copy(
            src_ref=give.at[k], dst_ref=part.at[k], send_sem=pair_send.at[0], recv_sem=pair_recv.at[0, k],
            device_id={"chan": partner}, device_id_type=MESH)

    def back(k, half):
        return pltpu.make_async_remote_copy(
            src_ref=gathered.at[k, half], dst_ref=gathered.at[k, half], send_sem=pair_send.at[1],
            recv_sem=pair_recv.at[1, k], device_id={"chan": partner}, device_id_type=MESH)

    def remote(src, dst, kind, q, odd, k, there):
        return pltpu.make_async_remote_copy(
            src_ref=src, dst_ref=dst, send_sem=send_sem.at[kind, q, odd], recv_sem=recv_sem.at[kind, q, k],
            device_id={"chan": there}, device_id_type=MESH)

    def toward(q, up, odd, k):
        there = me + teeth[q][2] if up else me - teeth[q][2]
        return remote(own.at[k, q], inward.at[0 if up else 1, k, q], IN_UP if up else IN_DOWN, q, odd, k, there)

    def onward(q, up, odd, k, src):
        there = me + spine[q][2] if up else me - spine[q][2]
        return remote(src, along.at[0 if up else 1, k, q], ON_UP if up else ON_DOWN, q, odd, k, there)

    def outward(q, up, odd, k):
        there = me + teeth[q][2] if up else me - teeth[q][2]
        block = gathered.at[k, core, q]
        return remote(block, block, OUT_UP if up else OUT_DOWN, q, odd, k, there)

    def prepare(block, k):
        for q in range(2):
            for m in range(many):
                s = ((k % per) * 2 + q) * many + m
                held = jnp.clip(src_ref[s] - me * nchan, 0, nchan - 1)
                mask = plane[s]
                give[k, q, m] = block[held, 1 - core] * mask
                own[k, q, m] = block[held, core] * mask
        across(k).start()

    def guarded(k, also, run):
        @pl.when((k >= 0) & (k < n) & also)
        def _():
            run()

    def enter(k, odd):
        across(k).wait_recv()
        own[k] = own[k] + part[k]
        for q in range(2):
            pos, length, _ = teeth[q]
            if root(q, odd) > 0:
                @pl.when(pos == 0)
                def _():
                    toward(q, True, odd, k).start()

            if root(q, odd) < length - 1:
                @pl.when(pos == length - 1)
                def _():
                    toward(q, False, odd, k).start()

    def relay_in(q, t, p):
        pos, length, _ = teeth[q]
        for up in (True, False):
            for here in range(1, length - 1):
                steps = here if up else length - 1 - here
                odd = (p - LAG * steps) % 2
                k = t - LAG * steps
                if (here < root(q, odd)) if up else (here > root(q, odd)):
                    def run():
                        toward(q, up, odd, k).wait_recv()
                        own[k, q] = own[k, q] + inward[0 if up else 1, k, q]
                        toward(q, up, odd, k).start()

                    guarded(k, pos == here, run)

    def reach_root(q, k, odd):
        length = teeth[q][1]
        at, span, _ = spine[q]
        ways = []
        if root(q, odd) > 0:
            ways.append(0)
        if root(q, odd) < length - 1:
            ways.append(1)
        for way in ways:
            toward(q, way == 0, odd, k).wait_recv()
        if ways:
            total = own[k, q]
            for way in ways:
                total = total + inward[way, k, q]
            own[k, q] = total
        if span > 1:
            @pl.when(at == 0)
            def _():
                onward(q, True, odd, k, own.at[k, q]).start()

            @pl.when(at == span - 1)
            def _():
                onward(q, False, odd, k, own.at[k, q]).start()

    def relay_on(q, t, p):
        at, span, _ = spine[q]
        for up in (True, False):
            for here in range(1, span - 1):
                steps = here if up else span - 1 - here
                odd = (p - LAG * steps) % 2
                k = t - LAG * steps

                def run():
                    way = 0 if up else 1
                    onward(q, up, odd, k, own.at[k, q]).wait_recv()
                    passed[way, k, q] = own[k, q] + along[way, k, q]
                    onward(q, up, odd, k, passed.at[way, k, q]).start()

                guarded(k, at_root[q][odd] & (at == here), run)

    def finish(q, k, odd):
        pos, length, _ = teeth[q]
        at, span, _ = spine[q]
        if span == 1:
            gathered[k, core, q] = own[k, q]
        else:
            @pl.when(at == 0)
            def _():
                onward(q, False, odd, k, own.at[k, q]).wait_recv()
                gathered[k, core, q] = own[k, q] + along[1, k, q]

            @pl.when(at == span - 1)
            def _():
                onward(q, True, odd, k, own.at[k, q]).wait_recv()
                gathered[k, core, q] = own[k, q] + along[0, k, q]

            if span > 2:
                @pl.when((at > 0) & (at < span - 1))
                def _():
                    gathered[k, core, q] = own[k, q] + along[0, k, q] + along[1, k, q]
        if root(q, odd) < length - 1:
            outward(q, True, odd, k).start()
        if root(q, odd) > 0:
            outward(q, False, odd, k).start()

    def spread(q, t, p):
        pos, length, _ = teeth[q]
        for far in range(reach[q], 0, -1):
            odd = (p - LAG * far) % 2
            k = t - LAG * far
            for up in (True, False):
                here = root(q, odd) + far if up else root(q, odd) - far
                if 0 <= here < length:
                    def run():
                        outward(q, up, odd, k).wait_recv()
                        if (here < length - 1) if up else (here > 0):
                            outward(q, up, odd, k).start()

                    guarded(k, pos == here, run)

    def all_sent():
        def drain(block, sem):
            pltpu.make_async_remote_copy(
                src_ref=block, dst_ref=block, send_sem=sem, recv_sem=pair_recv.at[0, 0],
                device_id={"chan": partner}, device_id_type=MESH).wait_send()

        drain(give, pair_send.at[0])
        drain(give, pair_send.at[1])
        for q in range(2):
            pos, length, _ = teeth[q]
            at, span, _ = spine[q]
            for odd in range(2):
                r = root(q, odd)
                for kind, when in ((IN_UP, pos < r), (IN_DOWN, pos > r),
                                   (ON_UP, (pos == r) & (at < span - 1)), (ON_DOWN, (pos == r) & (at > 0)),
                                   (OUT_UP, (pos >= r) & (pos < length - 1)), (OUT_DOWN, (pos <= r) & (pos > 0))):
                    @pl.when(when)
                    def _():
                        drain(own.at[pl.ds(0, n // 2), q], send_sem.at[kind, q, odd])

    sign = jnp.where(lax.broadcasted_iota(jnp.int32, (1, depth), 1) < nwin, -1.0, 1.0)

    def settle(k):
        base = ((k // per) % 2) * (2 * nsrc * pitch)
        back(k, 1 - core).wait_recv()
        for q in range(2):
            for m in range(many):
                both = jnp.concatenate([gathered[k, 0, q, m], gathered[k, 1, q, m]], axis=0)
                x = jnp.transpose(both).astype(jnp.float32)
                s = ((k % per) * 2 + q) * many + m
                src_t[pl.ds(base + s * pitch, FB)] = x
                src_t[pl.ds(base + (s + nsrc) * pitch, FB)] = pltpu.roll(x, nwin, axis=1) * sign

    def turn(k):
        b, lot = k // per, k % per
        base = (b % 3) * (nrow * pitch)
        count = nchan // per
        for u in range(count):
            c = lot * count + u
            x = jnp.transpose(spec[b, c].reshape(depth, FB)).astype(jnp.float32) * flags[pl.ds(c, 1)]
            chan_t[pl.ds(base + (c + HALO) * pitch, FB)] = x

    def turn_edges(b):
        from_neighbours([b])
        base = (b % 3) * (nrow * pitch)
        for h in range(2 * HALO):
            side, c = h // HALO, h % HALO
            row = halo_valid[side][(8 - HALO + c) if side == 0 else c][None].astype(jnp.float32)
            row = jnp.concatenate([row, row], axis=1)
            x = jnp.transpose(halo[side, b, c].reshape(depth, FB)).astype(jnp.float32) * row
            chan_t[pl.ds(base + (c + side * (HALO + nchan)) * pitch, FB)] = x

    def correlate(b, f):
        right = chan_t[pl.ds((b % 3) * (nrow * pitch) + f, nrow, stride=pitch)].astype(jnp.bfloat16)
        left = src_t[pl.ds((b % 2) * (2 * nsrc * pitch) + f, 2 * nsrc, stride=pitch)].astype(jnp.bfloat16)
        both = lax.dot_general(left, right, (((1,), (1,)), ((), ())), preferred_element_type=jnp.float32)
        cross_t[pl.ds((b % 2) * (FB * cpitch) + f * cpitch, 2 * nsrc), 0:nrow] = both

    ahead = (lax.broadcasted_iota(jnp.int32, (nchan, FB), 1)
             - lax.broadcasted_iota(jnp.int32, (nchan, FB), 0))
    band = ((ahead >= 0) & (ahead <= 2 * HALO)).astype(jnp.bfloat16)

    def smooth(b, s):
        base = (b % 2) * (FB * cpitch)
        re = cross_t[pl.ds(base + s, FB, stride=cpitch)]
        im = cross_t[pl.ds(base + s + nsrc, FB, stride=cpitch)]
        flat = jnp.concatenate([re, im], axis=0).astype(jnp.bfloat16)
        total = lax.dot_general(band, flat, (((1,), (1,)), ((), ())),
                                preferred_element_type=jnp.float32).astype(jnp.bfloat16)
        rows = pl.ds(pl.multiple_of(s * nchan, nchan), nchan)
        flat_ref[rows, pl.ds(pl.multiple_of(b * FB, FB), FB)] = total[:, 0:FB]
        flat_ref[rows, pl.ds(pl.multiple_of((nblk + b) * FB, FB), FB)] = total[:, FB:]

    load_first.wait()

    def prepare_first(k, carry):
        prepare(first, k)
        return carry

    lax.fori_loop(0, per, prepare_first, 0, unroll=True)

    @pl.when(me == 0)
    def _():
        halo[0] = jnp.zeros(halo.shape[1:], halo.dtype)
        halo_valid[0] = jnp.zeros(halo_valid.shape[1:], halo_valid.dtype)

    @pl.when(me == size - 1)
    def _():
        halo[1] = jnp.zeros(halo.shape[1:], halo.dtype)
        halo_valid[1] = jnp.zeros(halo_valid.shape[1:], halo_valid.dtype)

    def clear():
        def some(f, carry):
            cross_t[pl.ds(pl.multiple_of(f * 8 * cpitch, 8), 8 * cpitch)] = jnp.zeros((8 * cpitch, FB), jnp.float32)
            return carry

        lax.fori_loop(0, 2 * FB // 8, some, 0)
        for slot in range(3):
            for c in range(nchan + 2 * HALO, nrow):
                chan_t[pl.ds((slot * nrow + c) * pitch, pitch)] = jnp.zeros((pitch, depth), jnp.float32)

    def step(t, p):
        @pl.when(t == LOADED)
        def _():
            for b in range(nblk):
                load(b).wait()

        @pl.when(t == LOADED + 1)
        def _():
            clear()
            from_neighbours()

        for b in range(nblk):
            @pl.when(t == settled + per * (b + 1) - EARLY)
            def _():
                to_neighbours(lambda copy: copy.start(), [b])

        guarded(t - ENTER, True, functools.partial(enter, t - ENTER, (p - ENTER) % 2))
        for q in range(2):
            relay_in(q, t - ENTER, (p - ENTER) % 2)
        for q in range(2):
            odd = (p - rooted[q]) % 2
            guarded(t - rooted[q], at_root[q][odd], functools.partial(reach_root, q, t - rooted[q], odd))
        for q in range(2):
            relay_on(q, t - rooted[q], (p - rooted[q]) % 2)
        for q in range(2):
            odd = (p - summed[q]) % 2
            guarded(t - summed[q], at_root[q][odd], functools.partial(finish, q, t - summed[q], odd))
        for q in range(2):
            spread(q, t - summed[q], (p - summed[q]) % 2)
        guarded(t - spread_at, True, lambda: back(t - spread_at, core).start())
        guarded(t, t >= per, lambda: prepare(spec.at[t // per], t))
        guarded(t - turn_at, True, functools.partial(turn, t - turn_at))
        guarded(t - settled, True, functools.partial(settle, t - settled))

        for b in range(nblk):
            @pl.when(t == settled + per * (b + 1) - 1)
            def _():
                turn_edges(b)

        at = t - settled - per

        @pl.when((at >= 0) & (at < n - per))
        def _():
            b, lot = at // per, at % per
            for u in range(FB // per):
                correlate(b, lot * (FB // per) + u)

        also = at - per

        @pl.when((also >= 0) & (also < n - 2 * per))
        def _():
            b, lot = also // per, also % per
            for u in range(nsrc // per):
                smooth(b, lot * (nsrc // per) + u)

    def steps(tt, carry):
        for p in range(2):
            step(2 * tt + p, p)
        return carry

    lax.fori_loop(0, (n + settled + 1) // 2, steps, 0)

    def rest(u, carry):
        for v in range(32):
            correlate(nblk - 1, u * 32 + v)
        return carry

    lax.fori_loop(0, FB // 32, rest, 0)
    for b in range(max(nblk - 2, 0), nblk):
        def last(s, carry):
            smooth(b, s)
            return carry

        lax.fori_loop(0, nsrc, last, 0, unroll=4)
    all_sent()
    to_neighbours(lambda copy: copy.wait_send())
    to_neighbours(lambda copy: copy.wait_send(), range(nblk))


def lag_kernel(scale, flat_ref, table_ref, out_ref):
    lags = jnp.dot(flat_ref[...], table_ref[...], preferred_element_type=jnp.float32)
    out_ref[...] = lags * scale


def local(size, spectra, valid, sources):
    nchan, _, nwin, nbins = spectra.shape
    nsrc = sources.shape[0]
    depth, nlags = 2 * nwin, 2 * nbins
    vmem = pl.BlockSpec(memory_space=pltpu.VMEM)

    chips = size // 2
    inner = 1
    while (2 * inner) ** 2 <= chips and chips % (2 * inner) == 0:
        inner *= 2
    outer = chips // inner
    nblk = nbins // FB
    many = MANY
    n = nblk * nsrc // (2 * many)
    nrow = -(-(nchan + 2 * HALO) // 16) * 16
    pitch, cpitch = FB + 1, 2 * nsrc + 1
    chunks = lambda *lead: pltpu.VMEM(lead + (n, 2, many, nwin, FB), jnp.bfloat16)
    flat = pl.pallas_call(
        functools.partial(cross_kernel, outer, inner, nrow),
        out_shape=jax.ShapeDtypeStruct((nsrc * nchan, nlags), jnp.bfloat16),
        in_specs=[pl.BlockSpec(memory_space=pltpu.SMEM), vmem, pl.BlockSpec(memory_space=pltpu.MemorySpace.HBM)],
        out_specs=vmem,
        scratch_shapes=[pltpu.VMEM((nchan, 2, nwin, FB), jnp.bfloat16),
                        pltpu.VMEM((nblk, nchan, 2, nwin, FB), jnp.bfloat16),
                        pltpu.VMEM((2, nblk, HALO, 2, nwin, FB), jnp.bfloat16),
                        pltpu.VMEM((2, 8, nwin), jnp.int32),
                        pltpu.VMEM((nchan, depth), jnp.float32),
                        pltpu.VMEM((nsrc, nwin, FB), jnp.bfloat16),
                        chunks(), chunks(), chunks(), chunks(2), chunks(2), chunks(2),
                        pltpu.VMEM((n, 2, 2, many, nwin, FB), jnp.bfloat16),
                        pltpu.VMEM((3 * nrow * pitch, depth), jnp.float32),
                        pltpu.VMEM((2 * 2 * nsrc * pitch, depth), jnp.float32),
                        pltpu.VMEM((2 * FB * cpitch, FB), jnp.float32),
                        pltpu.SemaphoreType.DMA((1 + nblk,)),
                        pltpu.SemaphoreType.DMA((2,)), pltpu.SemaphoreType.DMA((2, n)),
                        pltpu.SemaphoreType.DMA((6, 2, 2)), pltpu.SemaphoreType.DMA((6, 2, n)),
                        pltpu.SemaphoreType.DMA((2, nblk + 1)), pltpu.SemaphoreType.DMA((2, nblk + 1))],
        compiler_params=pltpu.CompilerParams(
            collective_id=0, has_side_effects=True, vmem_limit_bytes=54 << 20),
        name="cross",
    )(sources, valid, spectra)

    rows = nsrc * nchan // 4
    lags = pl.pallas_call(
        functools.partial(lag_kernel, 1.0 / (nwin * (2 * HALO + 1.0))),
        grid=(4,),
        out_shape=jax.ShapeDtypeStruct((nsrc * nchan, nlags), jnp.float32),
        in_specs=[pl.BlockSpec((rows, nlags), lambda at: (at, 0)),
                  pl.BlockSpec((nlags, nlags), lambda at: (0, 0))],
        out_specs=pl.BlockSpec((rows, nlags), lambda at: (at, 0)),
        compiler_params=pltpu.CompilerParams(vmem_limit_bytes=24 << 20),
        name="lags",
    )(flat, jnp.asarray(make_table(nbins, nlags)))
    return lags.reshape(nsrc, nchan, nlags)


def solution(mesh):
    in_specs = (P(("grp", "chan"), None, None, None), P(("grp", "chan"), None), P("grp"))
    out_specs = P("grp", "chan", None)
    return jax.shard_map(functools.partial(local, mesh.shape["chan"]), mesh=mesh,
                         in_specs=in_specs, out_specs=out_specs, check_vma=False)
```

time: 75.5 us -> 58.4 us (0.77)
  Pallas kernels: 73.8 us -> 56.6 us
    pallas_call x1, Pallas kernels: 69.7 us -> 52.5 us  [local(): pl.pallas_call(functools.partial(cross_kernel, outer, inner, nrow), out_s...]
where the time goes in v2:
time: 58.4 us; the launch traced here: 58.2 us
  Pallas kernels  56.6 us (97%)
  local copies, waits for them, and re-layouts  1.59 us (3%)
    pallas_call x1, Pallas kernels, local(): pl.pallas_call(functools.partial(cross_kernel, outer, inner, nrow), out_s...  52.5 us
    pallas_call x1, Pallas kernels, local(): pl.pallas_call(functools.partial(lag_kernel, 1.0 / (nwin * (2 * HALO + 1....  4.08 us
    unnamed x4, local copies, waits for them, and re-layouts  1.59 us

profile of v2, /device:TPU:0, one launch (start us, length us, event | category | flops | bytes accessed | tf_op | source)
XLA Modules:
  0.0 58.2 jit_solution(12318720399268408723)
XLA Ops:
  0.0 0.0 copy-start.1
  0.0 52.5 %cross.1.flat_ref = bf16[1024,1024]{1,0:T(8,128)(2,1)} custom-call(s32[16]{0:T(128)} %src_ref.1, s32[64,64]{1,0:T(8,128)} %valid_ref.1, bf16[64,2,64,512]{3,2,1,0:T(8,128)(2,1)} %spec_ref.1), custom_call_target="tpu_custom_call" | custom-call | tf_op jit(solution)/shard_map/cross/pallas_call | solution.py:489
  52.5 0.0 copy-done.1
  52.5 0.0 copy-start
  52.6 1.6 %copy-done = bf16[1024,1024]{1,0:T(8,128)(2,1)S(1)} copy-done((bf16[1024,1024]{1,0:T(8,128)(2,1)S(1)}, bf16[1024,1024]{1,0:T(8,128)(2,1)}, u32[]{:S(2)}) %copy-start) | copy-done | bytes 2097176
  54.1 4.1 %lags.1 = f32[1024,1024]{1,0:T(8,128)} custom-call(bf16[1024,1024]{1,0:T(8,128)(2,1)S(1)} %copy-done, bf16[1024,1024]{1,0:T(8,128)(2,1)S(1)} %copy-done.1), custom_call_target="tpu_custom_call" | custom-call | tf_op jit(solution)/shard_map/lags/pallas_call | solution.py:515
Async XLA Ops:
  0.0 52.5 %copy-start.1 = (bf16[1024,1024]{1,0:T(8,128)(2,1)S(1)}, bf16[1024,1024]{1,0:T(8,128)(2,1)}, u32[]{:S(2)}) copy-start(bf16[1024,1024]{1,0:T(8,128)(2,1)} %constant.2.clone.table_ref) | copy-start | bytes 6291460
  52.5 1.6 %copy-start = (bf16[1024,1024]{1,0:T(8,128)(2,1)S(1)}, bf16[1024,1024]{1,0:T(8,128)(2,1)}, u32[]{:S(2)}) copy-start(bf16[1024,1024]{1,0:T(8,128)(2,1)} %cross.1.flat_ref) | copy-start | bytes 6291460

commit v3 on v2

--- a/solution.py
+++ b/solution.py
@@ -11,9 +11,8 @@
 MESH = pl.DeviceIdType.MESH
 HALO = 2
 LAG = 3
-ENTER = 2
+AHEAD = 2
 SETTLE = 2
-LOADED = 4
 EARLY = 5
 FB = 128
 MANY = 2
@@ -26,7 +25,9 @@
     angle = 2.0 * np.pi * phase / nlags
     weight = np.where(freq == 0, 1.0, 2.0) / nlags
     table = np.concatenate([weight[:, None] * np.cos(angle), -weight[:, None] * np.sin(angle)])
-    return table.astype(np.float32).astype(jnp.bfloat16)
+    order = np.concatenate([blk * FB + half * nbins + np.arange(odd, FB, 2)
+                            for odd in range(2) for blk in range(nbins // FB) for half in range(2)])
+    return table[order, :nlags // 2].astype(np.float32).astype(jnp.bfloat16)
 
 
 def cross_kernel(outer, inner, nrow, src_ref, valid_ref, spec_ref, flat_ref,
@@ -50,11 +51,12 @@
         return 0 if length == 1 else (length - 1) // 2 + odd
 
     reach = [max(root(q, 1), teeth[q][1] - 1 - root(q, 0)) for q in range(2)]
-    rooted = [ENTER + LAG * reach[q] for q in range(2)]
+    rooted = [LAG * reach[q] for q in range(2)]
     summed = [rooted[q] + LAG * (spine[q][1] - 1) for q in range(2)]
     spread_at = max(summed[q] + LAG * reach[q] for q in range(2))
     settled = spread_at + SETTLE
-    turn_at = settled - per
+    loaded = max(per - AHEAD, 0)
+    turn_at = min(loaded + 1, settled)
     at_root = [[teeth[q][0] == root(q, odd) for odd in range(2)] for q in range(2)]
 
     def load(b):
@@ -308,7 +310,6 @@
 
     def settle(k):
         base = ((k // per) % 2) * (2 * nsrc * pitch)
-        back(k, 1 - core).wait_recv()
         for q in range(2):
             for m in range(many):
                 both = jnp.concatenate([gathered[k, 0, q, m], gathered[k, 1, q, m]], axis=0)
@@ -319,7 +320,7 @@
 
     def turn(k):
         b, lot = k // per, k % per
-        base = (b % 3) * (nrow * pitch)
+        base = b * (nrow * pitch)
         count = nchan // per
         for u in range(count):
             c = lot * count + u
@@ -328,7 +329,7 @@
 
     def turn_edges(b):
         from_neighbours([b])
-        base = (b % 3) * (nrow * pitch)
+        base = b * (nrow * pitch)
         for h in range(2 * HALO):
             side, c = h // HALO, h % HALO
             row = halo_valid[side][(8 - HALO + c) if side == 0 else c][None].astype(jnp.float32)
@@ -337,7 +338,7 @@
             chan_t[pl.ds(base + (c + side * (HALO + nchan)) * pitch, FB)] = x
 
     def correlate(b, f):
-        right = chan_t[pl.ds((b % 3) * (nrow * pitch) + f, nrow, stride=pitch)].astype(jnp.bfloat16)
+        right = chan_t[pl.ds(b * (nrow * pitch) + f, nrow, stride=pitch)].astype(jnp.bfloat16)
         left = src_t[pl.ds((b % 2) * (2 * nsrc * pitch) + f, 2 * nsrc, stride=pitch)].astype(jnp.bfloat16)
         both = lax.dot_general(left, right, (((1,), (1,)), ((), ())), preferred_element_type=jnp.float32)
         cross_t[pl.ds((b % 2) * (FB * cpitch) + f * cpitch, 2 * nsrc), 0:nrow] = both
@@ -348,9 +349,9 @@
 
     def smooth(b, s):
         base = (b % 2) * (FB * cpitch)
-        re = cross_t[pl.ds(base + s, FB, stride=cpitch)]
-        im = cross_t[pl.ds(base + s + nsrc, FB, stride=cpitch)]
-        flat = jnp.concatenate([re, im], axis=0).astype(jnp.bfloat16)
+        parts = [cross_t[pl.ds(base + odd * cpitch + s + half * nsrc, FB // 2, stride=2 * cpitch)]
+                 for odd in range(2) for half in range(2)]
+        flat = jnp.concatenate(parts, axis=0).astype(jnp.bfloat16)
         total = lax.dot_general(band, flat, (((1,), (1,)), ((), ())),
                                 preferred_element_type=jnp.float32).astype(jnp.bfloat16)
         rows = pl.ds(pl.multiple_of(s * nchan, nchan), nchan)
@@ -381,17 +382,17 @@
             return carry
 
         lax.fori_loop(0, 2 * FB // 8, some, 0)
-        for slot in range(3):
+        for slot in range(nblk):
             for c in range(nchan + 2 * HALO, nrow):
                 chan_t[pl.ds((slot * nrow + c) * pitch, pitch)] = jnp.zeros((pitch, depth), jnp.float32)
 
     def step(t, p):
-        @pl.when(t == LOADED)
+        @pl.when(t == loaded)
         def _():
             for b in range(nblk):
                 load(b).wait()
 
-        @pl.when(t == LOADED + 1)
+        @pl.when(t == loaded + 1)
         def _():
             clear()
             from_neighbours()
@@ -401,9 +402,9 @@
             def _():
                 to_neighbours(lambda copy: copy.start(), [b])
 
-        guarded(t - ENTER, True, functools.partial(enter, t - ENTER, (p - ENTER) % 2))
-        for q in range(2):
-            relay_in(q, t - ENTER, (p - ENTER) % 2)
+        guarded(t, True, functools.partial(enter, t, p))
+        for q in range(2):
+            relay_in(q, t, p)
         for q in range(2):
             odd = (p - rooted[q]) % 2
             guarded(t - rooted[q], at_root[q][odd], functools.partial(reach_root, q, t - rooted[q], odd))
@@ -415,30 +416,30 @@
         for q in range(2):
             spread(q, t - summed[q], (p - summed[q]) % 2)
         guarded(t - spread_at, True, lambda: back(t - spread_at, core).start())
-        guarded(t, t >= per, lambda: prepare(spec.at[t // per], t))
+        later = t + AHEAD
+        guarded(later, later >= per, lambda: prepare(spec.at[later // per], later))
         guarded(t - turn_at, True, functools.partial(turn, t - turn_at))
-        guarded(t - settled, True, functools.partial(settle, t - settled))
-
         for b in range(nblk):
             @pl.when(t == settled + per * (b + 1) - 1)
             def _():
                 turn_edges(b)
 
-        at = t - settled - per
-
-        @pl.when((at >= 0) & (at < n - per))
-        def _():
-            b, lot = at // per, at % per
+        now = t - settled
+
+        @pl.when((now >= 0) & (now < per))
+        def _():
+            back(now, 1 - core).wait_recv()
+            settle(now)
+
+        @pl.when((now >= per) & (now < n))
+        def _():
+            back(now, 1 - core).wait_recv()
+            b, lot = now // per - 1, now % per
+            for u in range(nsrc // per):
+                smooth(jnp.maximum(b - 1, 0), lot * (nsrc // per) + u)
             for u in range(FB // per):
                 correlate(b, lot * (FB // per) + u)
-
-        also = at - per
-
-        @pl.when((also >= 0) & (also < n - 2 * per))
-        def _():
-            b, lot = also // per, also % per
-            for u in range(nsrc // per):
-                smooth(b, lot * (nsrc // per) + u)
+            settle(now)
 
     def steps(tt, carry):
         for p in range(2):
@@ -447,26 +448,23 @@
 
     lax.fori_loop(0, (n + settled + 1) // 2, steps, 0)
 
-    def rest(u, carry):
-        for v in range(32):
-            correlate(nblk - 1, u * 32 + v)
-        return carry
-
-    lax.fori_loop(0, FB // 32, rest, 0)
-    for b in range(max(nblk - 2, 0), nblk):
-        def last(s, carry):
-            smooth(b, s)
-            return carry
-
-        lax.fori_loop(0, nsrc, last, 0, unroll=4)
+    for s in range(nsrc if nblk > 1 else 0):
+        smooth(nblk - 2, s)
+    for f in range(FB):
+        correlate(nblk - 1, f)
+    for s in range(nsrc):
+        smooth(nblk - 1, s)
     all_sent()
     to_neighbours(lambda copy: copy.wait_send())
     to_neighbours(lambda copy: copy.wait_send(), range(nblk))
 
 
 def lag_kernel(scale, flat_ref, table_ref, out_ref):
-    lags = jnp.dot(flat_ref[...], table_ref[...], preferred_element_type=jnp.float32)
-    out_ref[...] = lags * scale
+    half = table_ref.shape[1]
+    even = jnp.dot(flat_ref[:, 0:half], table_ref[0:half], preferred_element_type=jnp.float32)
+    odd = jnp.dot(flat_ref[:, half:], table_ref[half:], preferred_element_type=jnp.float32)
+    out_ref[:, 0:half] = (even + odd) * scale
+    out_ref[:, half:] = (even - odd) * scale
 
 
 def local(size, spectra, valid, sources):
@@ -488,7 +486,7 @@
     chunks = lambda *lead: pltpu.VMEM(lead + (n, 2, many, nwin, FB), jnp.bfloat16)
     flat = pl.pallas_call(
         functools.partial(cross_kernel, outer, inner, nrow),
-        out_shape=jax.ShapeDtypeStruct((nsrc * nchan, nlags), jnp.bfloat16),
+        out_shape=pltpu.VMEM((nsrc * nchan, nlags), jnp.bfloat16),
         in_specs=[pl.BlockSpec(memory_space=pltpu.SMEM), vmem, pl.BlockSpec(memory_space=pltpu.MemorySpace.HBM)],
         out_specs=vmem,
         scratch_shapes=[pltpu.VMEM((nchan, 2, nwin, FB), jnp.bfloat16),
@@ -499,7 +497,7 @@
                         pltpu.VMEM((nsrc, nwin, FB), jnp.bfloat16),
                         chunks(), chunks(), chunks(), chunks(2), chunks(2), chunks(2),
                         pltpu.VMEM((n, 2, 2, many, nwin, FB), jnp.bfloat16),
-                        pltpu.VMEM((3 * nrow * pitch, depth), jnp.float32),
+                        pltpu.VMEM((nblk * nrow * pitch, depth), jnp.float32),
                         pltpu.VMEM((2 * 2 * nsrc * pitch, depth), jnp.float32),
                         pltpu.VMEM((2 * FB * cpitch, FB), jnp.float32),
                         pltpu.SemaphoreType.DMA((1 + nblk,)),
@@ -507,7 +505,7 @@
                         pltpu.SemaphoreType.DMA((6, 2, 2)), pltpu.SemaphoreType.DMA((6, 2, n)),
                         pltpu.SemaphoreType.DMA((2, nblk + 1)), pltpu.SemaphoreType.DMA((2, nblk + 1))],
         compiler_params=pltpu.CompilerParams(
-            collective_id=0, has_side_effects=True, vmem_limit_bytes=54 << 20),
+            collective_id=0, has_side_effects=True, vmem_limit_bytes=56 << 20),
         name="cross",
     )(sources, valid, spectra)
 
@@ -517,7 +515,7 @@
         grid=(4,),
         out_shape=jax.ShapeDtypeStruct((nsrc * nchan, nlags), jnp.float32),
         in_specs=[pl.BlockSpec((rows, nlags), lambda at: (at, 0)),
-                  pl.BlockSpec((nlags, nlags), lambda at: (0, 0))],
+                  pl.BlockSpec((nlags, nlags // 2), lambda at: (0, 0))],
         out_specs=pl.BlockSpec((rows, nlags), lambda at: (at, 0)),
         compiler_params=pltpu.CompilerParams(vmem_limit_bytes=24 << 20),
         name="lags",

time: 58.4 us -> 49.6 us (0.85)
  Pallas kernels: 56.6 us -> 49.5 us
  local copies, waits for them, and re-layouts: 1.59 us -> 0.01 us
    pallas_call x1, Pallas kernels: 52.5 us -> 46.1 us  [local(): pl.pallas_call(functools.partial(cross_kernel, outer, inner, nrow), out_s...]
    unnamed x4 -> x2, local copies, waits for them, and re-layouts: 1.59 us -> 0.01 us
    pallas_call x1, Pallas kernels: 4.08 us -> 3.34 us  [local(): pl.pallas_call(functools.partial(lag_kernel, 1.0 / (nwin * (2 * HALO + 1....]
where the time goes in v3:
time: 49.6 us; the launch traced here: 49.5 us
  Pallas kernels  49.5 us (100%)
    pallas_call x1, Pallas kernels, local(): pl.pallas_call(functools.partial(cross_kernel, outer, inner, nrow), out_s...  46.1 us
    pallas_call x1, Pallas kernels, local(): pl.pallas_call(functools.partial(lag_kernel, 1.0 / (nwin * (2 * HALO + 1....  3.34 us

profile of v3, /device:TPU:0, one launch (start us, length us, event | category | flops | bytes accessed | tf_op | source)
XLA Modules:
  0.0 49.5 jit_solution(12139539067706417579)
XLA Ops:
  0.0 0.0 copy-start
  0.0 46.1 %cross.1.flat_ref = bf16[1024,1024]{1,0:T(8,128)(2,1)S(1)} custom-call(s32[16]{0:T(128)} %src_ref.1, s32[64,64]{1,0:T(8,128)} %valid_ref.1, bf16[64,2,64,512]{3,2,1,0:T(8,128)(2,1)} %spec_ref.1), custom_call_target="tpu_custom_call" | custom-call | tf_op jit(solution)/shard_map/cross/pallas_call | solution.py:487
  46.1 0.0 copy-done
  46.1 3.3 %lags.1 = f32[1024,1024]{1,0:T(8,128)} custom-call(bf16[1024,1024]{1,0:T(8,128)(2,1)S(1)} %cross.1.flat_ref, bf16[1024,512]{1,0:T(8,128)(2,1)S(1)} %copy-done), custom_call_target="tpu_custom_call" | custom-call | tf_op jit(solution)/shard_map/lags/pallas_call | solution.py:513
Async XLA Ops:
  0.0 46.1 %copy-start = (bf16[1024,512]{1,0:T(8,128)(2,1)S(1)}, bf16[1024,512]{1,0:T(8,128)(2,1)}, u32[]{:S(2)}) copy-start(bf16[1024,512]{1,0:T(8,128)(2,1)} %constant.2.clone.table_ref) | copy-start | bytes 3145732

commit v4 on v3

--- a/solution.py
+++ b/solution.py
@@ -10,8 +10,10 @@
 
 MESH = pl.DeviceIdType.MESH
 HALO = 2
-LAG = 3
+HALF_LAG = 6
+FIRST_EDGES = 1
 AHEAD = 2
+PIECES = 8
 SETTLE = 2
 EARLY = 5
 FB = 128
@@ -30,7 +32,7 @@
     return table[order, :nlags // 2].astype(np.float32).astype(jnp.bfloat16)
 
 
-def cross_kernel(outer, inner, nrow, src_ref, valid_ref, spec_ref, flat_ref,
+def cross_kernel(outer, inner, nrow, src_hbm, valid_hbm, spec_ref, flat_ref, src_ref, valid_ref,
                  first, spec, halo, halo_valid, flags, plane, give, own, part, inward, along, passed, gathered,
                  chan_t, src_t, cross_t, load_sem, pair_send, pair_recv, send_sem, recv_sem, edge_send, edge_recv):
     nblk, nchan, _, nwin, _ = spec.shape
@@ -51,9 +53,13 @@
         return 0 if length == 1 else (length - 1) // 2 + odd
 
     reach = [max(root(q, 1), teeth[q][1] - 1 - root(q, 0)) for q in range(2)]
-    rooted = [LAG * reach[q] for q in range(2)]
-    summed = [rooted[q] + LAG * (spine[q][1] - 1) for q in range(2)]
-    spread_at = max(summed[q] + LAG * reach[q] for q in range(2))
+    rooted = reach
+    summed = [rooted[q] + spine[q][1] - 1 for q in range(2)]
+
+    def lag(hops):
+        return (HALF_LAG * hops + 1) // 2
+
+    spread_at = max(lag(summed[q] + reach[q]) for q in range(2))
     settled = spread_at + SETTLE
     loaded = max(per - AHEAD, 0)
     turn_at = min(loaded + 1, settled)
@@ -62,6 +68,10 @@
     def load(b):
         return pltpu.make_async_copy(spec_ref.at[:, :, :, pl.ds(b * FB, FB)], spec.at[b], load_sem.at[1 + b])
 
+    small = [pltpu.make_async_copy(src_hbm, src_ref, load_sem.at[1 + nblk]),
+             pltpu.make_async_copy(valid_hbm, valid_ref, load_sem.at[2 + nblk])]
+    for copy in small:
+        copy.start()
     load_first = pltpu.make_async_copy(spec_ref.at[:, :, :, pl.ds(0, FB)], first, load_sem.at[0])
     load_first.start()
     for b in range(nblk):
@@ -85,6 +95,8 @@
 
         count = count + (pos > 0).astype(jnp.int32) + (pos < length - 1).astype(jnp.int32)
 
+    for copy in small:
+        copy.wait()
     raw = valid_ref[...].astype(jnp.float32)
     flags[...] = jnp.concatenate([raw, raw], axis=1)
     by_window = jnp.transpose(flags[...])[0:nwin].astype(jnp.bfloat16)
@@ -132,6 +144,8 @@
                 copy.wait_recv()
 
     to_neighbours(lambda copy: copy.start())
+    if FIRST_EDGES:
+        to_neighbours(lambda copy: copy.start(), range(FIRST_EDGES))
 
     def across(k):
         return pltpu.make_async_remote_copy(
@@ -196,8 +210,8 @@
         for up in (True, False):
             for here in range(1, length - 1):
                 steps = here if up else length - 1 - here
-                odd = (p - LAG * steps) % 2
-                k = t - LAG * steps
+                odd = (p - lag(steps)) % 2
+                k = t - lag(steps)
                 if (here < root(q, odd)) if up else (here > root(q, odd)):
                     def run():
                         toward(q, up, odd, k).wait_recv()
@@ -235,8 +249,8 @@
         for up in (True, False):
             for here in range(1, span - 1):
                 steps = here if up else span - 1 - here
-                odd = (p - LAG * steps) % 2
-                k = t - LAG * steps
+                odd = (p - lag(rooted[q] + steps)) % 2
+                k = t - lag(rooted[q] + steps)
 
                 def run():
                     way = 0 if up else 1
@@ -274,8 +288,8 @@
     def spread(q, t, p):
         pos, length, _ = teeth[q]
         for far in range(reach[q], 0, -1):
-            odd = (p - LAG * far) % 2
-            k = t - LAG * far
+            odd = (p - lag(summed[q] + far)) % 2
+            k = t - lag(summed[q] + far)
             for up in (True, False):
                 here = root(q, odd) + far if up else root(q, odd) - far
                 if 0 <= here < length:
@@ -397,7 +411,7 @@
             clear()
             from_neighbours()
 
-        for b in range(nblk):
+        for b in range(FIRST_EDGES, nblk):
             @pl.when(t == settled + per * (b + 1) - EARLY)
             def _():
                 to_neighbours(lambda copy: copy.start(), [b])
@@ -406,15 +420,17 @@
         for q in range(2):
             relay_in(q, t, p)
         for q in range(2):
-            odd = (p - rooted[q]) % 2
-            guarded(t - rooted[q], at_root[q][odd], functools.partial(reach_root, q, t - rooted[q], odd))
-        for q in range(2):
-            relay_on(q, t - rooted[q], (p - rooted[q]) % 2)
-        for q in range(2):
-            odd = (p - summed[q]) % 2
-            guarded(t - summed[q], at_root[q][odd], functools.partial(finish, q, t - summed[q], odd))
-        for q in range(2):
-            spread(q, t - summed[q], (p - summed[q]) % 2)
+            at = lag(rooted[q])
+            odd = (p - at) % 2
+            guarded(t - at, at_root[q][odd], functools.partial(reach_root, q, t - at, odd))
+        for q in range(2):
+            relay_on(q, t, p)
+        for q in range(2):
+            at = lag(summed[q])
+            odd = (p - at) % 2
+            guarded(t - at, at_root[q][odd], functools.partial(finish, q, t - at, odd))
+        for q in range(2):
+            spread(q, t, p)
         guarded(t - spread_at, True, lambda: back(t - spread_at, core).start())
         later = t + AHEAD
         guarded(later, later >= per, lambda: prepare(spec.at[later // per], later))
@@ -459,12 +475,21 @@
     to_neighbours(lambda copy: copy.wait_send(), range(nblk))
 
 
-def lag_kernel(scale, flat_ref, table_ref, out_ref):
+def lag_kernel(scale, flat_ref, table_ref, out_ref, lags, sems):
     half = table_ref.shape[1]
-    even = jnp.dot(flat_ref[:, 0:half], table_ref[0:half], preferred_element_type=jnp.float32)
-    odd = jnp.dot(flat_ref[:, half:], table_ref[half:], preferred_element_type=jnp.float32)
-    out_ref[:, 0:half] = (even + odd) * scale
-    out_ref[:, half:] = (even - odd) * scale
+    rows = lags.shape[1]
+    copies = []
+    for piece in range(PIECES):
+        at = pl.ds(piece * rows, rows)
+        even = jnp.dot(flat_ref[at, 0:half], table_ref[0:half], preferred_element_type=jnp.float32)
+        odd = jnp.dot(flat_ref[at, half:], table_ref[half:], preferred_element_type=jnp.float32)
+        lags[piece, :, 0:half] = (even + odd) * scale
+        lags[piece, :, half:] = (even - odd) * scale
+        copy = pltpu.make_async_copy(lags.at[piece], out_ref.at[at], sems.at[piece])
+        copy.start()
+        copies.append(copy)
+    for copy in copies:
+        copy.wait()
 
 
 def local(size, spectra, valid, sources):
@@ -487,9 +512,10 @@
     flat = pl.pallas_call(
         functools.partial(cross_kernel, outer, inner, nrow),
         out_shape=pltpu.VMEM((nsrc * nchan, nlags), jnp.bfloat16),
-        in_specs=[pl.BlockSpec(memory_space=pltpu.SMEM), vmem, pl.BlockSpec(memory_space=pltpu.MemorySpace.HBM)],
+        in_specs=[pl.BlockSpec(memory_space=pltpu.MemorySpace.HBM)] * 3,
         out_specs=vmem,
-        scratch_shapes=[pltpu.VMEM((nchan, 2, nwin, FB), jnp.bfloat16),
+        scratch_shapes=[pltpu.SMEM((nsrc,), jnp.int32), pltpu.VMEM((nchan, nwin), jnp.int32),
+                        pltpu.VMEM((nchan, 2, nwin, FB), jnp.bfloat16),
                         pltpu.VMEM((nblk, nchan, 2, nwin, FB), jnp.bfloat16),
                         pltpu.VMEM((2, nblk, HALO, 2, nwin, FB), jnp.bfloat16),
                         pltpu.VMEM((2, 8, nwin), jnp.int32),
@@ -500,7 +526,7 @@
                         pltpu.VMEM((nblk * nrow * pitch, depth), jnp.float32),
                         pltpu.VMEM((2 * 2 * nsrc * pitch, depth), jnp.float32),
                         pltpu.VMEM((2 * FB * cpitch, FB), jnp.float32),
-                        pltpu.SemaphoreType.DMA((1 + nblk,)),
+                        pltpu.SemaphoreType.DMA((3 + nblk,)),
                         pltpu.SemaphoreType.DMA((2,)), pltpu.SemaphoreType.DMA((2, n)),
                         pltpu.SemaphoreType.DMA((6, 2, 2)), pltpu.SemaphoreType.DMA((6, 2, n)),
                         pltpu.SemaphoreType.DMA((2, nblk + 1)), pltpu.SemaphoreType.DMA((2, nblk + 1))],
@@ -509,14 +535,13 @@
         name="cross",
     )(sources, valid, spectra)
 
-    rows = nsrc * nchan // 4
+    rows = nsrc * nchan // PIECES
     lags = pl.pallas_call(
         functools.partial(lag_kernel, 1.0 / (nwin * (2 * HALO + 1.0))),
-        grid=(4,),
         out_shape=jax.ShapeDtypeStruct((nsrc * nchan, nlags), jnp.float32),
-        in_specs=[pl.BlockSpec((rows, nlags), lambda at: (at, 0)),
-                  pl.BlockSpec((nlags, nlags // 2), lambda at: (0, 0))],
-        out_specs=pl.BlockSpec((rows, nlags), lambda at: (at, 0)),
+        in_specs=[vmem, vmem],
+        out_specs=pl.BlockSpec(memory_space=pltpu.MemorySpace.HBM),
+        scratch_shapes=[pltpu.VMEM((PIECES, rows, nlags), jnp.float32), pltpu.SemaphoreType.DMA((PIECES,))],
         compiler_params=pltpu.CompilerParams(vmem_limit_bytes=24 << 20),
         name="lags",
     )(flat, jnp.asarray(make_table(nbins, nlags)))

time: 49.6 us -> 47.8 us (0.964)
  Pallas kernels: 49.5 us -> 47.4 us
    pallas_call x1, Pallas kernels: 46.1 us -> 45 us  [local(): pl.pallas_call(functools.partial(cross_kernel, outer, inner, nrow), out_s...]
    pallas_call x1, Pallas kernels: 3.34 us -> 2.42 us  [local(): pl.pallas_call(functools.partial(lag_kernel, 1.0 / (nwin * (2 * HALO + 1....]
where the time goes in v4:
time: 47.8 us; the launch traced here: 47.4 us
  Pallas kernels  47.4 us (99%)
    pallas_call x1, Pallas kernels, local(): pl.pallas_call(functools.partial(cross_kernel, outer, inner, nrow), out_s...  45 us
    pallas_call x1, Pallas kernels, local(): pl.pallas_call(functools.partial(lag_kernel, 1.0 / (nwin * (2 * HALO + 1....  2.42 us

profile of v4, /device:TPU:0, one launch (start us, length us, event | category | flops | bytes accessed | tf_op | source)
XLA Modules:
  0.0 47.4 jit_solution(5617616555118053730)
XLA Ops:
  0.0 0.0 copy-start
  0.0 45.0 %cross.1.flat_ref = bf16[1024,1024]{1,0:T(8,128)(2,1)S(1)} custom-call(s32[16]{0:T(128)} %src_hbm.1, s32[64,64]{1,0:T(8,128)} %valid_hbm.1, bf16[64,2,64,512]{3,2,1,0:T(8,128)(2,1)} %spec_ref.1), custom_call_target="tpu_custom_call" | custom-call | tf_op jit(solution)/shard_map/cross/pallas_call | solution.py:512
  45.0 0.0 copy-done
  45.0 2.4 %lags.1 = f32[1024,1024]{1,0:T(8,128)} custom-call(bf16[1024,1024]{1,0:T(8,128)(2,1)S(1)} %cross.1.flat_ref, bf16[1024,512]{1,0:T(8,128)(2,1)S(1)} %copy-done), custom_call_target="tpu_custom_call" | custom-call | tf_op jit(solution)/shard_map/lags/pallas_call | solution.py:539
Async XLA Ops:
  0.0 45.0 %copy-start = (bf16[1024,512]{1,0:T(8,128)(2,1)S(1)}, bf16[1024,512]{1,0:T(8,128)(2,1)}, u32[]{:S(2)}) copy-start(bf16[1024,512]{1,0:T(8,128)(2,1)} %constant.2.clone.table_ref) | copy-start | bytes 3145732

commit v5 on v4

--- a/solution.py
+++ b/solution.py
@@ -351,24 +351,39 @@
             x = jnp.transpose(halo[side, b, c].reshape(depth, FB)).astype(jnp.float32) * row
             chan_t[pl.ds(base + (c + side * (HALO + nchan)) * pitch, FB)] = x
 
+    nothing = jnp.zeros((2 * nsrc, depth), jnp.bfloat16)
+
     def correlate(b, f):
-        right = chan_t[pl.ds(b * (nrow * pitch) + f, nrow, stride=pitch)].astype(jnp.bfloat16)
-        left = src_t[pl.ds((b % 2) * (2 * nsrc * pitch) + f, 2 * nsrc, stride=pitch)].astype(jnp.bfloat16)
-        both = lax.dot_general(left, right, (((1,), (1,)), ((), ())), preferred_element_type=jnp.float32)
-        cross_t[pl.ds((b % 2) * (FB * cpitch) + f * cpitch, 2 * nsrc), 0:nrow] = both
+        def rows(ref, base, count, at):
+            return ref[pl.ds(base + at, count, stride=pitch)].astype(jnp.bfloat16)
+
+        right = [rows(chan_t, b * (nrow * pitch), nrow, f + u) for u in range(2)]
+        left = [rows(src_t, (b % 2) * (2 * nsrc * pitch), 2 * nsrc, f + u) for u in range(2)]
+        left = jnp.concatenate([jnp.concatenate([left[0], nothing], axis=1),
+                                jnp.concatenate([nothing, left[1]], axis=1)], axis=0)
+        both = lax.dot_general(left, jnp.concatenate(right, axis=1), (((1,), (1,)), ((), ())),
+                               preferred_element_type=jnp.float32)
+        for u in range(2):
+            at = (b % 2) * (FB * cpitch) + (f + u) * cpitch
+            cross_t[pl.ds(at, 2 * nsrc), 0:nrow] = both[2 * nsrc * u:2 * nsrc * (u + 1)]
 
     ahead = (lax.broadcasted_iota(jnp.int32, (nchan, FB), 1)
              - lax.broadcasted_iota(jnp.int32, (nchan, FB), 0))
     band = ((ahead >= 0) & (ahead <= 2 * HALO)).astype(jnp.bfloat16)
+    apart = jnp.zeros_like(band)
+    bands = jnp.concatenate([jnp.concatenate([band, apart], axis=1),
+                             jnp.concatenate([apart, band], axis=1)], axis=0)
 
     def smooth(b, s):
         base = (b % 2) * (FB * cpitch)
-        parts = [cross_t[pl.ds(base + odd * cpitch + s + half * nsrc, FB // 2, stride=2 * cpitch)]
-                 for odd in range(2) for half in range(2)]
-        flat = jnp.concatenate(parts, axis=0).astype(jnp.bfloat16)
-        total = lax.dot_general(band, flat, (((1,), (1,)), ((), ())),
+        flats = []
+        for u in range(2):
+            parts = [cross_t[pl.ds(base + odd * cpitch + s + u + half * nsrc, FB // 2, stride=2 * cpitch)]
+                     for odd in range(2) for half in range(2)]
+            flats.append(jnp.concatenate(parts, axis=0).astype(jnp.bfloat16))
+        total = lax.dot_general(bands, jnp.concatenate(flats, axis=1), (((1,), (1,)), ((), ())),
                                 preferred_element_type=jnp.float32).astype(jnp.bfloat16)
-        rows = pl.ds(pl.multiple_of(s * nchan, nchan), nchan)
+        rows = pl.ds(pl.multiple_of(s * nchan, nchan), 2 * nchan)
         flat_ref[rows, pl.ds(pl.multiple_of(b * FB, FB), FB)] = total[:, 0:FB]
         flat_ref[rows, pl.ds(pl.multiple_of((nblk + b) * FB, FB), FB)] = total[:, FB:]
 
@@ -423,6 +438,23 @@
             at = lag(rooted[q])
             odd = (p - at) % 2
             guarded(t - at, at_root[q][odd], functools.partial(reach_root, q, t - at, odd))
+        now = t - settled
+
+        @pl.when((now >= 0) & (now < per))
+        def _():
+            back(now, 1 - core).wait_recv()
+            settle(now)
+
+        @pl.when((now >= per) & (now < n))
+        def _():
+            back(now, 1 - core).wait_recv()
+            b, lot = now // per - 1, now % per
+            for u in range(0, nsrc // per, 2):
+                smooth(jnp.maximum(b - 1, 0), lot * (nsrc // per) + u)
+            for u in range(0, FB // per, 2):
+                correlate(b, lot * (FB // per) + u)
+            settle(now)
+
         for q in range(2):
             relay_on(q, t, p)
         for q in range(2):
@@ -440,22 +472,6 @@
             def _():
                 turn_edges(b)
 
-        now = t - settled
-
-        @pl.when((now >= 0) & (now < per))
-        def _():
-            back(now, 1 - core).wait_recv()
-            settle(now)
-
-        @pl.when((now >= per) & (now < n))
-        def _():
-            back(now, 1 - core).wait_recv()
-            b, lot = now // per - 1, now % per
-            for u in range(nsrc // per):
-                smooth(jnp.maximum(b - 1, 0), lot * (nsrc // per) + u)
-            for u in range(FB // per):
-                correlate(b, lot * (FB // per) + u)
-            settle(now)
 
     def steps(tt, carry):
         for p in range(2):
@@ -464,11 +480,11 @@
 
     lax.fori_loop(0, (n + settled + 1) // 2, steps, 0)
 
-    for s in range(nsrc if nblk > 1 else 0):
+    for s in range(0, nsrc if nblk > 1 else 0, 2):
         smooth(nblk - 2, s)
-    for f in range(FB):
+    for f in range(0, FB, 2):
         correlate(nblk - 1, f)
-    for s in range(nsrc):
+    for s in range(0, nsrc, 2):
         smooth(nblk - 1, s)
     all_sent()
     to_neighbours(lambda copy: copy.wait_send())

time: 47.8 us -> 46 us (0.962)
  Pallas kernels: 47.4 us -> 45.9 us
    pallas_call x1, Pallas kernels: 45 us -> 43.4 us  [local(): pl.pallas_call(functools.partial(cross_kernel, outer, inner, nrow), out_s...]
where the time goes in v5:
time: 46 us; the launch traced here: 45.9 us
  Pallas kernels  45.9 us (100%)
    pallas_call x1, Pallas kernels, local(): pl.pallas_call(functools.partial(cross_kernel, outer, inner, nrow), out_s...  43.4 us
    pallas_call x1, Pallas kernels, local(): pl.pallas_call(functools.partial(lag_kernel, 1.0 / (nwin * (2 * HALO + 1....  2.42 us

profile of v5, /device:TPU:0, one launch (start us, length us, event | category | flops | bytes accessed | tf_op | source)
XLA Modules:
  0.0 45.9 jit_solution(2794325727357819025)
XLA Ops:
  0.0 0.0 copy-start
  0.0 43.4 %cross.1.flat_ref = bf16[1024,1024]{1,0:T(8,128)(2,1)S(1)} custom-call(s32[16]{0:T(128)} %src_hbm.1, s32[64,64]{1,0:T(8,128)} %valid_hbm.1, bf16[64,2,64,512]{3,2,1,0:T(8,128)(2,1)} %spec_ref.1), custom_call_target="tpu_custom_call" | custom-call | tf_op jit(solution)/shard_map/cross/pallas_call | solution.py:528
  43.4 0.0 copy-done
  43.5 2.4 %lags.1 = f32[1024,1024]{1,0:T(8,128)} custom-call(bf16[1024,1024]{1,0:T(8,128)(2,1)S(1)} %cross.1.flat_ref, bf16[1024,512]{1,0:T(8,128)(2,1)S(1)} %copy-done), custom_call_target="tpu_custom_call" | custom-call | tf_op jit(solution)/shard_map/lags/pallas_call | solution.py:555
Async XLA Ops:
  0.0 43.4 %copy-start = (bf16[1024,512]{1,0:T(8,128)(2,1)S(1)}, bf16[1024,512]{1,0:T(8,128)(2,1)}, u32[]{:S(2)}) copy-start(bf16[1024,512]{1,0:T(8,128)(2,1)} %constant.2.clone.table_ref) | copy-start | bytes 3145732

commit v6 on v5

--- a/solution.py
+++ b/solution.py
@@ -478,7 +478,10 @@
             step(2 * tt + p, p)
         return carry
 
-    lax.fori_loop(0, (n + settled + 1) // 2, steps, 0)
+    total = n + settled
+    lax.fori_loop(0, total // 2, steps, 0)
+    if total % 2:
+        step(jnp.int32(total - 1), (total - 1) % 2)
 
     for s in range(0, nsrc if nblk > 1 else 0, 2):
         smooth(nblk - 2, s)

time: 46 us -> 45.6 us (level)
  Pallas kernels: 45.9 us -> 45.4 us
where the time goes in v6:
time: 45.6 us; the launch traced here: 45.4 us
  Pallas kernels  45.4 us (100%)
    pallas_call x1, Pallas kernels, local(): pl.pallas_call(functools.partial(cross_kernel, outer, inner, nrow), out_s...  43 us
    pallas_call x1, Pallas kernels, local(): pl.pallas_call(functools.partial(lag_kernel, 1.0 / (nwin * (2 * HALO + 1....  2.42 us

profile of v6, /device:TPU:0, one launch (start us, length us, event | category | flops | bytes accessed | tf_op | source)
XLA Modules:
  0.0 45.4 jit_solution(8554311972754282296)
XLA Ops:
  0.0 0.0 copy-start
  0.0 43.0 %cross.1.flat_ref = bf16[1024,1024]{1,0:T(8,128)(2,1)S(1)} custom-call(s32[16]{0:T(128)} %src_hbm.1, s32[64,64]{1,0:T(8,128)} %valid_hbm.1, bf16[64,2,64,512]{3,2,1,0:T(8,128)(2,1)} %spec_ref.1), custom_call_target="tpu_custom_call" | custom-call | tf_op jit(solution)/shard_map/cross/pallas_call | solution.py:531
  43.0 0.0 copy-done
  43.0 2.4 %lags.1 = f32[1024,1024]{1,0:T(8,128)} custom-call(bf16[1024,1024]{1,0:T(8,128)(2,1)S(1)} %cross.1.flat_ref, bf16[1024,512]{1,0:T(8,128)(2,1)S(1)} %copy-done), custom_call_target="tpu_custom_call" | custom-call | tf_op jit(solution)/shard_map/lags/pallas_call | solution.py:558
Async XLA Ops:
  0.0 43.0 %copy-start = (bf16[1024,512]{1,0:T(8,128)(2,1)S(1)}, bf16[1024,512]{1,0:T(8,128)(2,1)}, u32[]{:S(2)}) copy-start(bf16[1024,512]{1,0:T(8,128)(2,1)} %constant.2.clone.table_ref) | copy-start | bytes 3145732

commit v7 on v6

--- a/solution.py
+++ b/solution.py
@@ -525,7 +525,7 @@
     nblk = nbins // FB
     many = MANY
     n = nblk * nsrc // (2 * many)
-    nrow = -(-(nchan + 2 * HALO) // 16) * 16
+    nrow = -(-(nchan + 2 * HALO) // 8) * 8
     pitch, cpitch = FB + 1, 2 * nsrc + 1
     chunks = lambda *lead: pltpu.VMEM(lead + (n, 2, many, nwin, FB), jnp.bfloat16)
     flat = pl.pallas_call(

time: 45.6 us -> 45.6 us (level)
  no operation moved by 1% of the time
where the time goes in v7:
time: 45.6 us; the launch traced here: 45.5 us
  Pallas kernels  45.4 us (100%)
    pallas_call x1, Pallas kernels, local(): pl.pallas_call(functools.partial(cross_kernel, outer, inner, nrow), out_s...  43 us
    pallas_call x1, Pallas kernels, local(): pl.pallas_call(functools.partial(lag_kernel, 1.0 / (nwin * (2 * HALO + 1....  2.42 us

profile of v7, /device:TPU:0, one launch (start us, length us, event | category | flops | bytes accessed | tf_op | source)
XLA Modules:
  0.0 45.5 jit_solution(18316193202695026308)
XLA Ops:
  0.0 0.0 copy-start
  0.0 43.0 %cross.1.flat_ref = bf16[1024,1024]{1,0:T(8,128)(2,1)S(1)} custom-call(s32[16]{0:T(128)} %src_hbm.1, s32[64,64]{1,0:T(8,128)} %valid_hbm.1, bf16[64,2,64,512]{3,2,1,0:T(8,128)(2,1)} %spec_ref.1), custom_call_target="tpu_custom_call" | custom-call | tf_op jit(solution)/shard_map/cross/pallas_call | solution.py:531
  43.0 0.0 copy-done
  43.0 2.4 %lags.1 = f32[1024,1024]{1,0:T(8,128)} custom-call(bf16[1024,1024]{1,0:T(8,128)(2,1)S(1)} %cross.1.flat_ref, bf16[1024,512]{1,0:T(8,128)(2,1)S(1)} %copy-done), custom_call_target="tpu_custom_call" | custom-call | tf_op jit(solution)/shard_map/lags/pallas_call | solution.py:558
Async XLA Ops:
  0.0 43.0 %copy-start = (bf16[1024,512]{1,0:T(8,128)(2,1)S(1)}, bf16[1024,512]{1,0:T(8,128)(2,1)}, u32[]{:S(2)}) copy-start(bf16[1024,512]{1,0:T(8,128)(2,1)} %constant.2.clone.table_ref) | copy-start | bytes 3145732
